TPU v7x, 32 devices: a whole 2x2x4 slice. The times are simulated.
32 devices in a mesh: shard: 4 (over y, core), replica: 8 (over z, x).
Axes of the slice: x: 2, y: 2, z: 4, core: 2. Of those that a mesh axis runs over, the one named last changes fastest.
Arguments:
- tokens: bfloat16 [8, 1024, 1024], P('replica', 'shard'), may hold values from -6 to 6
- cotangent: bfloat16 [8, 1024, 1024], P('replica', 'shard'), may hold values from -6 to 6
- lengths: int32 [8], P('replica'), may hold values from 256 to 1024, as said below
- block_order: int32 [8, 8], P('replica'), may hold values from 0 to 7, as said below
- norm1_gain: bfloat16 [1024], P('shard'), may hold values from 0.099609375 to 1.8984375
- query_weight: bfloat16 [1024, 2048], P('shard'), may hold values from -0.1875 to 0.1875
- key_weight: bfloat16 [1024, 1024], P('shard'), may hold values from -0.1875 to 0.1875
- value_weight: bfloat16 [1024, 1024], P('shard'), may hold values from -0.1875 to 0.1875
- output_weight: bfloat16 [2048, 1024], P('shard'), may hold values from -1.5 to 1.5
- query_gain: bfloat16 [128], P('shard'), may hold values from 0.099609375 to 1.8984375
- key_gain: bfloat16 [128], P('shard'), may hold values from 0.099609375 to 1.8984375
- norm2_gain: bfloat16 [1024], P('shard'), may hold values from 0.099609375 to 1.8984375
- gate_weight: bfloat16 [1024, 3072], P('shard'), may hold values from -0.1875 to 0.1875
- up_weight: bfloat16 [1024, 3072], P('shard'), may hold values from -0.1875 to 0.1875
- down_weight: bfloat16 [3072, 1024], P('shard'), may hold values from -0.109375 to 0.109375
Outputs:
- output: bfloat16 [8, 1024, 1024], P('replica', 'shard')
- input_grad: float32 [8, 1024, 1024], P('replica', 'shard')
- norm1_gain_grad: float32 [1024], P('shard')
- query_weight_grad: float32 [1024, 2048], P('shard')
- key_weight_grad: float32 [1024, 1024], P('shard')
- value_weight_grad: float32 [1024, 1024], P('shard')
- output_weight_grad: float32 [2048, 1024], P('shard')
- query_gain_grad: float32 [128], P('shard')
- key_gain_grad: float32 [128], P('shard')
- norm2_gain_grad: float32 [1024], P('shard')
- gate_weight_grad: float32 [1024, 3072], P('shard')
- up_weight_grad: float32 [1024, 3072], P('shard')
- down_weight_grad: float32 [3072, 1024], P('shard')
Inputs may be any that keep to these rules, and one draw needn't show every extreme that they name: `lengths`: in every group of 1 sequence one has 1024 valid tokens; valid tokens hold positions 0 to length - 1. `block_order`: each row is a permutation of 0 to 7 in which places 2j and 2j + 1 hold blocks that add up to 7.
All inputs are finite; a program needn't handle non-finite values.
Results may differ from a plain program's by a relative error of at most 0.013.
Values may be sent and summed in bfloat16 or wider, within the bound.
A program may use at most 256 MiB of HBM per device.

v0:
```python
import jax
import jax.numpy as jnp
from jax import lax
from jax.sharding import PartitionSpec as P

EPSILON = 1e-06
ROPE_BASE = 1000000.0


def rms_scale(values, gain_vec):
    return (
        values * lax.rsqrt(jnp.mean(values * values, axis=-1, keepdims=True) + EPSILON) * gain_vec
    )


def rotate_half(values, cosine, sine_table):
    middle = values.shape[-1] // 2
    turned = jnp.concatenate([-values[..., middle:], values[..., :middle]], axis=-1)
    return values * cosine + turned * sine_table


def rotary_tables(position, head_width):
    middle = head_width // 2
    exponent = jnp.arange(middle, dtype=jnp.float32) * 2.0 / head_width
    inverse = ROPE_BASE ** (-exponent)
    phases = position.astype(jnp.float32)[..., None] * inverse
    phases = jnp.concatenate([phases, phases], axis=-1)
    return (jnp.cos(phases), jnp.sin(phases))


def turn_heads(query_raw, key_raw, query_scale, key_scale, cosine, sine_table):
    return (
        rotate_half(rms_scale(query_raw, query_scale), cosine, sine_table),
        rotate_half(rms_scale(key_raw, key_scale), cosine, sine_table),
    )


def swish_product(gate_proj, up_proj):
    return jax.nn.silu(gate_proj) * up_proj


def project(left, right):
    return jnp.einsum("sri,io->sro", left, right, preferred_element_type=jnp.float32)


def project_back(grad_rows, right):
    return jnp.einsum("sro,io->sri", grad_rows, right, preferred_element_type=jnp.float32)


def weight_grad(left, grad_rows):
    return jnp.einsum("sri,sro->io", left, grad_rows, preferred_element_type=jnp.float32)


def shards(
    tokens,
    cotangent,
    lengths,
    block_order,
    norm1_gain,
    query_weight,
    key_weight,
    value_weight,
    output_weight,
    query_gain,
    key_gain,
    norm2_gain,
    gate_weight,
    up_weight,
    down_weight,
):
    seq_count, row_count, model_width = tokens.shape
    shard_count = lax.axis_size("shard")
    block_count = block_order.shape[1]
    slot_len = row_count * shard_count
    block_len = slot_len // block_count
    head_width = query_gain.shape[0] * shard_count
    attn_parts = (
        lax.all_gather(norm1_gain, "shard", axis=0, tiled=True),
        lax.all_gather(query_weight, "shard", axis=0, tiled=True),
        lax.all_gather(key_weight, "shard", axis=0, tiled=True),
        lax.all_gather(value_weight, "shard", axis=0, tiled=True),
        lax.all_gather(output_weight, "shard", axis=0, tiled=True),
        lax.all_gather(query_gain, "shard", axis=0, tiled=True),
        lax.all_gather(key_gain, "shard", axis=0, tiled=True),
    )
    ffn_parts = (
        lax.all_gather(norm2_gain, "shard", axis=0, tiled=True),
        lax.all_gather(gate_weight, "shard", axis=0, tiled=True),
        lax.all_gather(up_weight, "shard", axis=0, tiled=True),
        lax.all_gather(down_weight, "shard", axis=0, tiled=True),
    )
    gain_one, w_query, w_key, w_value, w_output, gain_query, gain_key = attn_parts
    gain_two, w_gate, w_up, w_down = ffn_parts
    head_count = w_query.shape[1] // head_width
    group_count = w_key.shape[1] // head_width
    per_group = head_count // group_count
    score_scale = head_width ** (-0.5)
    offsets = jnp.arange(slot_len, dtype=jnp.int32)
    pos_all = (
        jnp.repeat(block_order, block_len, axis=1, total_repeat_length=slot_len) * block_len
        + offsets % block_len
    )
    pos_local = lax.dynamic_slice_in_dim(
        pos_all, lax.axis_index("shard") * row_count, row_count, axis=1
    )
    valid_rows = (pos_local < lengths[:, None]).astype(jnp.float32)[..., None]
    allowed = pos_all[:, None, None, None, :] <= pos_local[:, None, None, :, None]
    inputs = tokens.astype(jnp.float32)
    normed_f, norm_one_back = jax.vjp(rms_scale, inputs, gain_one.astype(jnp.float32))
    normed = normed_f.astype(jnp.bfloat16)
    query_raw = project(normed, w_query).reshape(seq_count, row_count, head_count, head_width)
    key_raw = project(normed, w_key).reshape(seq_count, row_count, group_count, head_width)
    value_local = project(normed, w_value).astype(jnp.bfloat16)
    cosine, sine_table = rotary_tables(pos_local, head_width)
    cosine = cosine[:, :, None, :]
    sine_table = sine_table[:, :, None, :]
    turned, turn_back = jax.vjp(
        lambda query_in, key_in, query_scale, key_scale: turn_heads(
            query_in, key_in, query_scale, key_scale, cosine, sine_table
        ),
        query_raw,
        key_raw,
        gain_query.astype(jnp.float32),
        gain_key.astype(jnp.float32),
    )
    queries = (
        turned[0]
        .astype(jnp.bfloat16)
        .reshape(seq_count, row_count, group_count, per_group, head_width)
    )
    key_local = (
        turned[1].astype(jnp.bfloat16).reshape(seq_count, row_count, group_count * head_width)
    )
    key_all, value_all = (
        lax.all_gather(key_local, "shard", axis=1, tiled=True),
        lax.all_gather(value_local, "shard", axis=1, tiled=True),
    )
    key_all = key_all.reshape(seq_count, slot_len, group_count, head_width)
    value_all = value_all.reshape(seq_count, slot_len, group_count, head_width)

    def scores_of():
        raw_scores = (
            jnp.einsum("srkgd,stkd->skgrt", queries, key_all, preferred_element_type=jnp.float32)
            * score_scale
        )
        return jnp.where(allowed, raw_scores, -1e30)

    scores = scores_of()
    row_top = jnp.max(scores, axis=-1, keepdims=True)
    log_total = row_top + jnp.log(jnp.sum(jnp.exp(scores - row_top), axis=-1, keepdims=True))
    softmax_b = jnp.exp(scores - log_total).astype(jnp.bfloat16)
    mixed_heads = jnp.einsum(
        "skgrt,stkd->srkgd", softmax_b, value_all, preferred_element_type=jnp.float32
    )
    mixed_heads = mixed_heads.reshape(seq_count, row_count, head_count * head_width).astype(
        jnp.bfloat16
    )
    hidden = inputs + project(mixed_heads, w_output)
    normed2_f, norm_two_back = jax.vjp(rms_scale, hidden, gain_two.astype(jnp.float32))
    normed2 = normed2_f.astype(jnp.bfloat16)
    active_f, swish_back = jax.vjp(swish_product, project(normed2, w_gate), project(normed2, w_up))
    active = active_f.astype(jnp.bfloat16)
    result = valid_rows * (hidden + project(active, w_down))
    output = result.astype(jnp.bfloat16)
    w_query, w_key, w_value, w_output = (
        lax.all_gather(query_weight, "shard", axis=0, tiled=True),
        lax.all_gather(key_weight, "shard", axis=0, tiled=True),
        lax.all_gather(value_weight, "shard", axis=0, tiled=True),
        lax.all_gather(output_weight, "shard", axis=0, tiled=True),
    )
    w_gate, w_up, w_down = (
        lax.all_gather(gate_weight, "shard", axis=0, tiled=True),
        lax.all_gather(up_weight, "shard", axis=0, tiled=True),
        lax.all_gather(down_weight, "shard", axis=0, tiled=True),
    )
    grad_result = cotangent.astype(jnp.float32) * valid_rows
    grad_branch = grad_result.astype(jnp.bfloat16)
    grad_gate_f, grad_up_f = swish_back(project_back(grad_branch, w_down))
    grad_gate_b = grad_gate_f.astype(jnp.bfloat16)
    grad_up_b = grad_up_f.astype(jnp.bfloat16)
    grad_hidden_norm, grad_gain_two = norm_two_back(
        project_back(grad_gate_b, w_gate) + project_back(grad_up_b, w_up)
    )
    grad_hidden = grad_result + grad_hidden_norm
    grad_mixed_in = grad_hidden.astype(jnp.bfloat16)
    grad_mixed = project_back(grad_mixed_in, w_output).astype(jnp.bfloat16)
    grad_mixed = grad_mixed.reshape(seq_count, row_count, group_count, per_group, head_width)
    softmax_f = jnp.exp(scores_of() - log_total)
    softmax_again = softmax_f.astype(jnp.bfloat16)
    grad_softmax = jnp.einsum(
        "srkgd,stkd->skgrt", grad_mixed, value_all, preferred_element_type=jnp.float32
    )
    grad_value_all = jnp.einsum(
        "skgrt,srkgd->stkd", softmax_again, grad_mixed, preferred_element_type=jnp.float32
    )
    row_inner = jnp.sum(softmax_f * grad_softmax, axis=-1, keepdims=True)
    grad_scores = (softmax_f * (grad_softmax - row_inner)).astype(jnp.bfloat16)
    grad_queries = (
        jnp.einsum("skgrt,stkd->srkgd", grad_scores, key_all, preferred_element_type=jnp.float32)
        * score_scale
    )
    grad_key_all = (
        jnp.einsum("skgrt,srkgd->stkd", grad_scores, queries, preferred_element_type=jnp.float32)
        * score_scale
    )
    grad_key_local, grad_value_local = (
        lax.psum_scatter(
            grad_key_all.reshape(seq_count, slot_len, group_count * head_width),
            "shard",
            scatter_dimension=1,
            tiled=True,
        ),
        lax.psum_scatter(
            grad_value_all.reshape(seq_count, slot_len, group_count * head_width),
            "shard",
            scatter_dimension=1,
            tiled=True,
        ),
    )
    grad_query_raw, grad_key_raw, grad_gain_query, grad_gain_key = turn_back(
        (
            grad_queries.reshape(seq_count, row_count, head_count, head_width),
            grad_key_local.reshape(seq_count, row_count, group_count, head_width),
        )
    )
    grad_query_b = grad_query_raw.reshape(seq_count, row_count, head_count * head_width).astype(
        jnp.bfloat16
    )
    grad_key_b = grad_key_raw.reshape(seq_count, row_count, group_count * head_width).astype(
        jnp.bfloat16
    )
    grad_value_b = grad_value_local.astype(jnp.bfloat16)
    grad_normed = (
        project_back(grad_query_b, w_query)
        + project_back(grad_key_b, w_key)
        + project_back(grad_value_b, w_value)
    )
    grad_inputs_norm, grad_gain_one = norm_one_back(grad_normed)
    input_grad = grad_hidden + grad_inputs_norm
    grad_down = weight_grad(active, grad_branch)
    grad_gate = weight_grad(normed2, grad_gate_b)
    grad_up = weight_grad(normed2, grad_up_b)
    grad_output_w = weight_grad(mixed_heads, grad_mixed_in)
    grad_query = weight_grad(normed, grad_query_b)
    grad_key = weight_grad(normed, grad_key_b)
    grad_value = weight_grad(normed, grad_value_b)
    shares = (
        lax.psum_scatter(grad_gain_one, "shard", scatter_dimension=0, tiled=True),
        lax.psum_scatter(grad_query, "shard", scatter_dimension=0, tiled=True),
        lax.psum_scatter(grad_key, "shard", scatter_dimension=0, tiled=True),
        lax.psum_scatter(grad_value, "shard", scatter_dimension=0, tiled=True),
        lax.psum_scatter(grad_output_w, "shard", scatter_dimension=0, tiled=True),
        lax.psum_scatter(grad_gain_query, "shard", scatter_dimension=0, tiled=True),
        lax.psum_scatter(grad_gain_key, "shard", scatter_dimension=0, tiled=True),
        lax.psum_scatter(grad_gain_two, "shard", scatter_dimension=0, tiled=True),
        lax.psum_scatter(grad_gate, "shard", scatter_dimension=0, tiled=True),
        lax.psum_scatter(grad_up, "shard", scatter_dimension=0, tiled=True),
        lax.psum_scatter(grad_down, "shard", scatter_dimension=0, tiled=True),
    )
    totals = lax.psum(
        (
            shares[0],
            shares[1],
            shares[2],
            shares[3],
            shares[4],
            shares[5],
            shares[6],
            shares[7],
            shares[8],
            shares[9],
            shares[10],
        ),
        "replica",
    )
    return (
        output,
        input_grad,
        totals[0],
        totals[1],
        totals[2],
        totals[3],
        totals[4],
        totals[5],
        totals[6],
        totals[7],
        totals[8],
        totals[9],
        totals[10],
    )


def solution(mesh):
    placed = (
        P("replica", "shard", None),
        P("replica", "shard", None),
        P("replica"),
        P("replica", None),
        P("shard"),
        P("shard", None),
        P("shard", None),
        P("shard", None),
        P("shard", None),
        P("shard"),
        P("shard"),
        P("shard"),
        P("shard", None),
        P("shard", None),
        P("shard", None),
    )
    return jax.shard_map(
        shards,
        mesh=mesh,
        in_specs=placed,
        out_specs=(
            P("replica", "shard", None),
            P("replica", "shard", None),
            P("shard"),
            P("shard", None),
            P("shard", None),
            P("shard", None),
            P("shard", None),
            P("shard"),
            P("shard"),
            P("shard"),
            P("shard", None),
            P("shard", None),
            P("shard", None),
        ),
        check_vma=False,
    )
```

profile of v0, /device:TPU:0, one launch (start us, length us, event | category | flops | bytes accessed | tf_op | source)
XLA Modules:
  0.0 1537.5 jit_solution(6394896684259161288)
XLA Ops:
  11.0 4.5 compare_select_fusion.1
  20.7 8.6 all-reduce.13
  29.9 5.1 all-gather.2
  43.5 15.7 %all-gather.14.cloned.1.call-done = bf16[1024,1024]{1,0:T(8,128)(2,1)} async-done(((bf16[256,1024]{1,0:T(8,128)(2,1)}), bf16[1024,1024]{1,0:T(8,128)(2,1)}) %all-gather.14.cloned.1.call-update) | async-done | bytes 2097168 | tf_op jit(solution)/shard_map/all_gather | solution.py:81
  65.3 5.4 all-gather.3
  70.9 13.1 all-gather.30.cloned.1.call-done
  89.1 30.9 %all-gather.18.cloned.1.call-done = bf16[1024,2048]{1,0:T(8,128)(2,1)} async-done(((bf16[256,2048]{1,0:T(8,128)(2,1)}), bf16[1024,2048]{1,0:T(8,128)(2,1)}) %all-gather.18.cloned.1.call-update) | async-done | bytes 4194320 | tf_op jit(solution)/shard_map/all_gather | solution.py:79
  119.9 4.0 fusion.87
  124.2 20.4 %all-gather.28.cloned.1.call-done = bf16[1024,1024]{1,0:T(8,128)(2,1)} async-done(((bf16[256,1024]{1,0:T(8,128)(2,1)}), bf16[1024,1024]{1,0:T(8,128)(2,1)}) %all-gather.28.cloned.1.call-update) | async-done | bytes 2097168 | tf_op jit(solution)/shard_map/all_gather | solution.py:136
  149.1 8.8 fusion.98
  157.8 8.0 exponential_reduce_fusion
  166.5 8.3 fusion.22
  174.9 5.6 all-gather.20.cloned.1.call-done
  180.5 3.6 multiply_reduce_fusion.4
  184.2 44.2 %all-gather.22.cloned.1.call-done = bf16[1024,3072]{1,0:T(8,128)(2,1)} async-done(((bf16[256,3072]{1,0:T(8,128)(2,1)}), bf16[1024,3072]{1,0:T(8,128)(2,1)}) %all-gather.22.cloned.1.call-update) | async-done | bytes 6291472 | tf_op jit(solution)/shard_map/all_gather | solution.py:88
  228.4 6.3 fusion.99
  234.7 41.7 %all-gather.24.cloned.1.call-done = bf16[1024,3072]{1,0:T(8,128)(2,1)} async-done(((bf16[256,3072]{1,0:T(8,128)(2,1)}), bf16[1024,3072]{1,0:T(8,128)(2,1)}) %all-gather.24.cloned.1.call-update) | async-done | bytes 6291472 | tf_op jit(solution)/shard_map/all_gather | solution.py:89
  276.4 6.3 fusion.100
  282.7 41.7 %all-gather.26.cloned.1.call-done = bf16[3072,1024]{1,0:T(8,128)(2,1)} async-done(((bf16[768,1024]{1,0:T(8,128)(2,1)}), bf16[3072,1024]{1,0:T(8,128)(2,1)}) %all-gather.26.cloned.1.call-update) | async-done | bytes 6291472 | tf_op jit(solution)/shard_map/all_gather | solution.py:90
  324.4 9.9 multiply_convert_fusion
  334.4 5.8 fusion.101
  347.1 14.5 fusion
  364.5 10.1 fusion.5
  374.6 8.3 bitcast_multiply_fusion.1
  384.1 11.4 fusion.10
  397.1 4.6 convolution_multiply_fusion
  406.8 4.7 fusion.85
  411.6 16.0 %reduce-scatter.10.cloned.1.call-done = f32[1,256,1024]{1,2,0:T(8,128)} async-done(((f32[1,1024,1024]{1,2,0:T(8,128)}), f32[1,256,1024]{1,2,0:T(8,128)}) %reduce-scatter.10.cloned.1.call-update) | async-done | bytes 1048592 | tf_op jit(solution)/shard_map/reduce_scatter | solution.py:207
  436.2 3.3 fusion.51
  439.6 35.2 %reduce-scatter.12.cloned.1.call-done = f32[1,256,1024]{1,2,0:T(8,128)} async-done(((f32[1,1024,1024]{1,2,0:T(8,128)}), f32[1,256,1024]{1,2,0:T(8,128)}) %reduce-scatter.12.cloned.1.call-update) | async-done | bytes 1048592 | tf_op jit(solution)/shard_map/reduce_scatter | solution.py:213
  474.8 4.1 fusion.54
  480.5 5.6 fusion.57
  486.1 8.8 fusion.103
  495.0 8.1 fusion.104
  504.2 7.9 fusion.66
  512.2 36.8 %reduce-scatter.14.cloned.1.call-done = f32[256,2048]{1,0:T(8,128)} async-done(((f32[1024,2048]{1,0:T(8,128)}), f32[256,2048]{1,0:T(8,128)}) %reduce-scatter.14.cloned.1.call-update) | async-done | bytes 2097168 | tf_op jit(solution)/shard_map/reduce_scatter | solution.py:249
  549.0 47.2 %reduce-scatter.16.cloned.1.call-done = f32[256,1024]{1,0:T(8,128)} async-done(((f32[1024,1024]{1,0:T(8,128)}), f32[256,1024]{1,0:T(8,128)}) %reduce-scatter.16.cloned.1.call-update) | async-done | bytes 1048592 | tf_op jit(solution)/shard_map/reduce_scatter | solution.py:250
  596.3 46.9 %reduce-scatter.18.cloned.1.call-done = f32[256,1024]{1,0:T(8,128)} async-done(((f32[1024,1024]{1,0:T(8,128)}), f32[256,1024]{1,0:T(8,128)}) %reduce-scatter.18.cloned.1.call-update) | async-done | bytes 1048592 | tf_op jit(solution)/shard_map/reduce_scatter | solution.py:251
  643.2 74.4 %reduce-scatter.20.cloned.1.call-done = f32[512,1024]{1,0:T(8,128)} async-done(((f32[2048,1024]{1,0:T(8,128)}), f32[512,1024]{1,0:T(8,128)}) %reduce-scatter.20.cloned.1.call-update) | async-done | bytes 2097168 | tf_op jit(solution)/shard_map/reduce_scatter | solution.py:252
  717.5 101.6 %reduce-scatter.22.cloned.1.call-done = f32[256,3072]{1,0:T(8,128)} async-done(((f32[1024,3072]{1,0:T(8,128)}), f32[256,3072]{1,0:T(8,128)}) %reduce-scatter.22.cloned.1.call-update) | async-done | bytes 3145744 | tf_op jit(solution)/shard_map/reduce_scatter | solution.py:256
  819.1 101.5 %reduce-scatter.24.cloned.1.call-done = f32[256,3072]{1,0:T(8,128)} async-done(((f32[1024,3072]{1,0:T(8,128)}), f32[256,3072]{1,0:T(8,128)}) %reduce-scatter.24.cloned.1.call-update) | async-done | bytes 3145744 | tf_op jit(solution)/shard_map/reduce_scatter | solution.py:257
  920.6 101.6 %reduce-scatter.26.cloned.1.call-done = f32[768,1024]{1,0:T(8,128)} async-done(((f32[3072,1024]{1,0:T(8,128)}), f32[768,1024]{1,0:T(8,128)}) %reduce-scatter.26.cloned.1.call-update) | async-done | bytes 3145744 | tf_op jit(solution)/shard_map/reduce_scatter | solution.py:258
  1023.6 3.6 fusion.102
  1027.3 5.6 fusion.29
  1036.8 6.3 all-reduce.12
  1043.4 22.8 %all-reduce.10 = (f32[256]{0:T(256)}, f32[32]{0:T(128)}, f32[32]{0:T(128)}, f32[256]{0:T(256)}) all-reduce(f32[256]{0:T(256)S(1)} %dynamic-slice.9, f32[32]{0:T(128)S(1)} %dynamic-slice.11, f32[32]{0:T(128)S(1)} %dynamic-slice.13, f32[256]{0:T(256)S(1)} %dynamic-slice.15), channel_id=1, replica_groups=mesh['shard'=4,'replica'=8] {'replica'}, use_global_device_ids=true, to_apply=%region_15.16 | all-reduce | flops 576 | bytes 4608 | tf_op jit(solution)/shard_map/psum | solution.py:260
  1067.5 448.0 %all-reduce.16.cloned.1.call-done = (f32[256,2048]{1,0:T(8,128)}, f32[256,1024]{1,0:T(8,128)}, f32[256,1024]{1,0:T(8,128)}, f32[512,1024]{1,0:T(8,128)}, f32[256...) async-done(((f32[256,2048]{1,0:T(8,128)}, f32[256,1024]{1,0:T(8,128)}, f32[256,1024]{1,0:T(8,128)}, f32[512,1024]{1,0:T(8,128)}, f32[256,3072]{1,0:T(8,128)}, ...) | async-done | bytes 15728656 | tf_op jit(solution)/shard_map/psum | solution.py:260
  1515.4 3.3 copy.180
  (266 shorter events, 79.3 us)
Async XLA Ops:
  7.2 29.2 %all-gather.16.cloned.1.call-start = ((), (), s32[]{:S(2)}) async-start(), calls=%async_computation.10 | async-start | bytes 2621440 | tf_op jit(solution)/shard_map/all_gather | solution.py:80
  7.9 51.3 %all-gather.14.cloned.1.call-start = ((), (), s32[]{:S(2)}) async-start(), calls=%async_computation.9 | async-start | bytes 2621440 | tf_op jit(solution)/shard_map/all_gather | solution.py:81
  8.7 75.3 %all-gather.30.cloned.1.call-start = ((), (), s32[]{:S(2)}) async-start(), calls=%async_computation.26 | async-start | bytes 2621440 | tf_op jit(solution)/shard_map/all_gather | solution.py:135
  16.8 130.6 %copy-start.29 = (f32[256,128]{0,1:T(8,128)}, f32[256,128]{0,1:T(8,128)S(1)}, u32[]{:S(2)}) copy-start(f32[256,128]{0,1:T(8,128)S(1)} %get-tuple-element.67) | copy-start | bytes 393220
  16.8 130.6 %copy-start.31 = (f32[256,128]{0,1:T(8,128)}, f32[256,128]{0,1:T(8,128)S(1)}, u32[]{:S(2)}) copy-start(f32[256,128]{0,1:T(8,128)S(1)} %get-tuple-element.68) | copy-start | bytes 393220
  16.9 23.9 %copy-start.40 = (f32[256,128]{1,0:T(8,128)}, f32[256,128]{1,0:T(8,128)S(1)}, u32[]{:S(2)}) copy-start(f32[256,128]{1,0:T(8,128)S(1)} %copy.101) | copy-start | bytes 393220
  29.2 10.5 copy-start.56
  35.1 5.8 copy-start.42
  41.3 17.9 %copy-start.3 = (bf16[1,256,1024]{2,1,0:T(8,128)(2,1)S(1)}, bf16[1,256,1024]{2,1,0:T(8,128)(2,1)}, u32[]{:S(2)}) copy-start(bf16[1,256,1024]{2,1,0:T(8,128)(2,1)} %param.17) | copy-start | bytes 1572868
  42.9 77.0 %all-gather.18.cloned.1.call-start = ((), (), s32[]{:S(2)}) async-start(), calls=%async_computation.11 | async-start | bytes 5242880 | tf_op jit(solution)/shard_map/all_gather | solution.py:79
  43.4 101.1 %all-gather.28.cloned.1.call-start = ((), (), s32[]{:S(2)}) async-start(), calls=%async_computation.25 | async-start | bytes 2621440 | tf_op jit(solution)/shard_map/all_gather | solution.py:136
  62.4 118.1 %all-gather.20.cloned.1.call-start = ((), (), s32[]{:S(2)}) async-start(), calls=%async_computation.12 | async-start | bytes 5242880 | tf_op jit(solution)/shard_map/all_gather | solution.py:82
  63.0 165.5 %all-gather.22.cloned.1.call-start = ((), (), s32[]{:S(2)}) async-start(), calls=%async_computation.13 | async-start | bytes 7864320 | tf_op jit(solution)/shard_map/all_gather | solution.py:88
  63.7 212.7 %all-gather.24.cloned.1.call-start = ((), (), s32[]{:S(2)}) async-start(), calls=%async_computation.14 | async-start | bytes 7864320 | tf_op jit(solution)/shard_map/all_gather | solution.py:89
  64.5 259.9 %all-gather.26.cloned.1.call-start = ((), (), s32[]{:S(2)}) async-start(), calls=%async_computation.15 | async-start | bytes 7864320 | tf_op jit(solution)/shard_map/all_gather | solution.py:90
  65.2 362.4 %reduce-scatter.10.cloned.1.call-start = ((), (), s32[]{:S(2)}) async-start(), calls=%async_computation.16 | async-start | bytes 5242880 | tf_op jit(solution)/shard_map/reduce_scatter | solution.py:207
  65.3 82.1 %copy-start.58 = (f32[128]{0:T(128)}, f32[128]{0:T(128)S(1)}, u32[]{:S(2)}) copy-start(f32[128]{0:T(128)S(1)} %convert_element_type.136) | copy-start | bytes 1540
  123.9 23.5 %copy-start = (f32[256,2048]{0,1:T(8,128)}, f32[256,2048]{0,1:T(8,128)S(1)}, u32[]{:S(2)}) copy-start(f32[256,2048]{0,1:T(8,128)S(1)} %fusion.87) | copy-start | bytes 6291460
  124.1 23.0 %copy-start.50 = (f32[256,16]{0,1:T(8,128)}, f32[256,16]{0,1:T(8,128)S(1)}, u32[]{:S(2)}) copy-start(f32[256,16]{0,1:T(8,128)S(1)} %multiply_reduce_fusion.2) | copy-start | bytes 49156
  124.1 23.0 %copy-start.48 = (f32[256,16]{0,1:T(8,128)}, f32[256,16]{0,1:T(8,128)S(1)}, u32[]{:S(2)}) copy-start(f32[256,16]{0,1:T(8,128)S(1)} %fusion.72) | copy-start | bytes 49156
  146.7 19.2 %copy-start.2 = (bf16[128,8,8,128]{3,2,1,0:T(8,128)(2,1)}, bf16[128,8,8,128]{3,2,1,0:T(8,128)(2,1)S(1)}, u32[]{:S(2)}) copy-start(bf16[128,8,8,128]{3,2,1,0:T(8,128)(2,1)S(1)} %copy.142) | copy-start | bytes 6291460
  149.1 8.8 copy-start.8
  174.8 9.2 copy-start.11
  184.0 159.1 %copy-start.19 = (f32[1,256,1024]{2,1,0:T(8,128)}, f32[1,256,1024]{2,1,0:T(8,128)S(1)}, u32[]{:S(2)}) copy-start(f32[1,256,1024]{2,1,0:T(8,128)S(1)} %get-tuple-element.82) | copy-start | bytes 3145732
  234.7 89.7 %copy-start.34 = (bf16[1,256,1024]{2,1,0:T(8,128)(2,1)S(1)}, bf16[1,256,1024]{2,1,0:T(8,128)(2,1)}, u32[]{:S(2)}) copy-start(bf16[1,256,1024]{2,1,0:T(8,128)(2,1)} %param.18) | copy-start | bytes 1572868
  334.3 5.8 copy-start.39
  334.3 5.8 copy-start.38
  334.3 5.8 copy-start.63
  340.2 4.3 copy-start.64
  347.1 14.6 slice-start
  347.1 15.0 slice-start.1
  347.1 16.2 %slice-start.2 = ((s8[16777216]{0:T(1024)(128)(4,1)}), s8[4194304]{0:T(1024)(128)(4,1)S(1)}, s32[]{:S(2)}) async-start(s8[16777216]{0:T(1024)(128)(4,1)} %bitcast.257), calls=%async_computation.30 | async-start | bytes 8388608
  347.1 17.4 %slice-start.3 = ((s8[16777216]{0:T(1024)(128)(4,1)}), s8[4194304]{0:T(1024)(128)(4,1)S(1)}, s32[]{:S(2)}) async-start(s8[16777216]{0:T(1024)(128)(4,1)} %bitcast.257), calls=%async_computation.31 | async-start | bytes 8388608
  364.4 10.1 copy-start.9
  382.9 91.9 %reduce-scatter.12.cloned.1.call-start = ((), (), s32[]{:S(2)}) async-start(), calls=%async_computation.17 | async-start | bytes 5242880 | tf_op jit(solution)/shard_map/reduce_scatter | solution.py:213
  395.5 6.2 copy-start.32
  395.5 153.5 %reduce-scatter.14.cloned.1.call-start = ((), (), s32[]{:S(2)}) async-start(), calls=%async_computation.18 | async-start | bytes 10485760 | tf_op jit(solution)/shard_map/reduce_scatter | solution.py:249
  411.5 18.6 %copy-start.41 = (f32[256,128]{1,0:T(8,128)S(1)}, f32[256,128]{1,0:T(8,128)}, u32[]{:S(2)}) copy-start(f32[256,128]{1,0:T(8,128)} %copy-done.40) | copy-start | bytes 393220
  411.6 184.7 %reduce-scatter.16.cloned.1.call-start = ((), (), s32[]{:S(2)}) async-start(), calls=%async_computation.19 | async-start | bytes 5242880 | tf_op jit(solution)/shard_map/reduce_scatter | solution.py:250
  439.6 203.6 %reduce-scatter.18.cloned.1.call-start = ((), (), s32[]{:S(2)}) async-start(), calls=%async_computation.20 | async-start | bytes 5242880 | tf_op jit(solution)/shard_map/reduce_scatter | solution.py:251
  478.9 238.6 %reduce-scatter.20.cloned.1.call-start = ((), (), s32[]{:S(2)}) async-start(), calls=%async_computation.21 | async-start | bytes 10485760 | tf_op jit(solution)/shard_map/reduce_scatter | solution.py:252
  486.1 333.0 %reduce-scatter.22.cloned.1.call-start = ((), (), s32[]{:S(2)}) async-start(), calls=%async_computation.22 | async-start | bytes 15728640 | tf_op jit(solution)/shard_map/reduce_scatter | solution.py:256
  494.9 425.7 %reduce-scatter.24.cloned.1.call-start = ((), (), s32[]{:S(2)}) async-start(), calls=%async_computation.23 | async-start | bytes 15728640 | tf_op jit(solution)/shard_map/reduce_scatter | solution.py:257
  503.2 519.0 %reduce-scatter.26.cloned.1.call-start = ((), (), s32[]{:S(2)}) async-start(), calls=%async_computation.24 | async-start | bytes 15728640 | tf_op jit(solution)/shard_map/reduce_scatter | solution.py:258
  512.1 1003.3 %all-reduce.16.cloned.1.call-start = ((), (), s32[]{:S(2)}) async-start(), calls=%async_computation.27 | async-start | bytes 31457280 | tf_op jit(solution)/shard_map/psum | solution.py:260
  1027.3 5.6 copy-start.16
  1027.3 5.6 copy-start.18
  1035.7 30.4 %copy-start.55 = (f32[256]{0:T(256)S(1)}, f32[256]{0:T(256)}, u32[]{:S(2)}) copy-start(f32[256]{0:T(256)} %copy-done.54) | copy-start | bytes 3076
  (41 other events, 79.5 us)
Sparse Core Ops, SparseCore 0:
  9.6 25.4 all-gather.15
  36.6 22.5 all-gather.13
  61.4 22.5 all-gather.29
  85.4 34.4 all-gather.17
  121.9 22.5 all-gather.27
  145.9 34.4 all-gather.19
  182.0 46.3 all-gather.21
  230.0 46.3 all-gather.23
  278.0 46.3 all-gather.25
  383.0 44.4 reduce-scatter.9
  430.3 44.5 reduce-scatter.11
  477.3 71.7 reduce-scatter.13
  551.7 44.5 reduce-scatter.15
  598.6 44.4 reduce-scatter.17
  645.8 71.7 reduce-scatter.19
  720.0 99.0 reduce-scatter.21
  821.5 99.0 reduce-scatter.23
  923.1 99.0 reduce-scatter.25
  1027.9 487.4 all-reduce.15
where the time goes:
time: 1540 us
  waiting for transfers between devices  1230 us (80%)
  matrix products  155 us (10%)
  blocking collectives  48.1 us (3%)
  local copies, waits for them, and re-layouts  47.8 us (3%)
  other arithmetic  39.9 us (3%)
  between operations  18.2 us (1%)
    psum x1, waiting for transfers between devices, shards(): lax.psum((shares[0], shares[1], shares[2], shares[3], shares[4], shares[5...  448 us
    reduce_scatter x1, waiting for transfers between devices, shards(): lax.psum_scatter(grad_down, 'shard', scatter_dimension=0, tiled=True)  102 us
    reduce_scatter x1, waiting for transfers between devices, shards(): lax.psum_scatter(grad_gate, 'shard', scatter_dimension=0, tiled=True)  102 us
    reduce_scatter x1, waiting for transfers between devices, shards(): lax.psum_scatter(grad_up, 'shard', scatter_dimension=0, tiled=True)  102 us
    reduce_scatter x1, waiting for transfers between devices, shards(): lax.psum_scatter(grad_output_w, 'shard', scatter_dimension=0, tiled=True)  74.4 us
    reduce_scatter x1, waiting for transfers between devices, shards(): lax.psum_scatter(grad_key, 'shard', scatter_dimension=0, tiled=True)  47.2 us
    reduce_scatter x1, waiting for transfers between devices, shards(): lax.psum_scatter(grad_value, 'shard', scatter_dimension=0, tiled=True)  46.9 us
    all_gather x1, waiting for transfers between devices, shards(): lax.all_gather(gate_weight, 'shard', axis=0, tiled=True)  44.2 us
  transfers between devices with their start and end apart: 19, of which 18 were waited for; matrix products, arithmetic and copies ran while one was open for 10% of the time, Pallas kernels for 0%

commit v1 on v0

v1 whole, which is shorter than its diff:
```python
import jax
import jax.numpy as jnp
from jax import lax
from jax.sharding import PartitionSpec as P

EPSILON = 1e-06
ROPE_BASE = 1000000.0
BF = jnp.bfloat16
F32 = jnp.float32


def rms_scale(values, gain_vec):
    return (
        values * lax.rsqrt(jnp.mean(values * values, axis=-1, keepdims=True) + EPSILON) * gain_vec
    )


def rotate_half(values, cosine, sine_table):
    middle = values.shape[-1] // 2
    turned = jnp.concatenate([-values[..., middle:], values[..., :middle]], axis=-1)
    return values * cosine + turned * sine_table


def rotary_tables(position, head_width):
    middle = head_width // 2
    exponent = jnp.arange(middle, dtype=F32) * 2.0 / head_width
    inverse = ROPE_BASE ** (-exponent)
    phases = position.astype(F32)[..., None] * inverse
    phases = jnp.concatenate([phases, phases], axis=-1)
    return (jnp.cos(phases), jnp.sin(phases))


def mm(a, b):
    return jnp.einsum("ri,io->ro", a, b, preferred_element_type=F32)


def mm_t(a, b):
    return jnp.einsum("ro,io->ri", a, b, preferred_element_type=F32)


def mm_w(a, b):
    return jnp.einsum("ri,ro->io", a, b, preferred_element_type=F32)


def gather_rows(v):
    return lax.all_gather(v, "shard", axis=0, tiled=True)


def scatter_rows(v):
    return lax.psum_scatter(v.astype(BF), "shard", scatter_dimension=0, tiled=True).astype(F32)


def to_columns(w):
    return lax.all_to_all(w, "shard", split_axis=1, concat_axis=0, tiled=True)


def to_rows(g):
    return lax.all_to_all(g, "shard", split_axis=0, concat_axis=1, tiled=True)


def shards(
    tokens,
    cotangent,
    lengths,
    block_order,
    norm1_gain,
    query_weight,
    key_weight,
    value_weight,
    output_weight,
    query_gain,
    key_gain,
    norm2_gain,
    gate_weight,
    up_weight,
    down_weight,
):
    shard_count = lax.axis_size("shard")
    row_count = tokens.shape[1]
    block_count = block_order.shape[1]
    slot_len = row_count * shard_count
    block_len = slot_len // block_count
    head_width = query_gain.shape[0] * shard_count
    score_scale = head_width ** (-0.5)
    gains = lax.all_gather(
        jnp.concatenate([norm1_gain, norm2_gain, query_gain, key_gain]), "shard", axis=0
    )
    wide = norm1_gain.shape[0]
    gain_one = gains[:, :wide].reshape(-1).astype(F32)
    gain_two = gains[:, wide : 2 * wide].reshape(-1).astype(F32)
    gain_query = gains[:, 2 * wide : 2 * wide + query_gain.shape[0]].reshape(-1).astype(F32)
    gain_key = gains[:, 2 * wide + query_gain.shape[0] :].reshape(-1).astype(F32)
    w_qkv = tuple(to_columns(w) for w in (query_weight, key_weight, value_weight))
    w_gate, w_up = to_columns(gate_weight), to_columns(up_weight)
    heads = w_qkv[0].shape[1] // head_width
    kvs = w_qkv[1].shape[1] // head_width
    per = heads // kvs

    offsets = jnp.arange(slot_len, dtype=jnp.int32)
    pos_all = (
        jnp.repeat(block_order[0], block_len, total_repeat_length=slot_len) * block_len
        + offsets % block_len
    )
    pos_local = lax.dynamic_slice_in_dim(pos_all, lax.axis_index("shard") * row_count, row_count)
    valid_rows = (pos_local < lengths[0]).astype(F32)[:, None]
    allowed = pos_all[None, None, None, :] <= pos_all[None, None, :, None]

    inputs = tokens[0].astype(F32)
    normed_f, norm_one_back = jax.vjp(rms_scale, inputs, gain_one)
    normed = gather_rows(normed_f.astype(BF))
    grad_result = cotangent[0].astype(F32) * valid_rows
    grad_branch = gather_rows(grad_result.astype(BF))
    query_raw = mm(normed, w_qkv[0]).reshape(slot_len, heads, head_width)
    key_raw = mm(normed, w_qkv[1]).reshape(slot_len, kvs, head_width)
    value = mm(normed, w_qkv[2]).astype(BF).reshape(slot_len, kvs, head_width)
    cosine, sine = rotary_tables(pos_all, head_width)
    cosine, sine = cosine[:, None, :], sine[:, None, :]

    def turn(q, k, gq, gk):
        return (
            rotate_half(rms_scale(q, gq), cosine, sine),
            rotate_half(rms_scale(k, gk), cosine, sine),
        )

    turned, turn_back = jax.vjp(turn, query_raw, key_raw, gain_query, gain_key)
    query = turned[0].astype(BF).reshape(slot_len, kvs, per, head_width)
    key = turned[1].astype(BF)

    def scores_of():
        raw = jnp.einsum("rkgd,tkd->kgrt", query, key, preferred_element_type=F32) * score_scale
        return jnp.where(allowed, raw, -1e30)

    scores = scores_of()
    row_top = jnp.max(scores, axis=-1, keepdims=True)
    log_total = row_top + jnp.log(jnp.sum(jnp.exp(scores - row_top), axis=-1, keepdims=True))
    probs = jnp.exp(scores - log_total).astype(BF)
    mixed = jnp.einsum("kgrt,tkd->rkgd", probs, value, preferred_element_type=F32)
    mixed = mixed.reshape(slot_len, heads * head_width).astype(BF)
    hidden = inputs + scatter_rows(mm(mixed, output_weight))
    normed2_f, norm_two_back = jax.vjp(rms_scale, hidden, gain_two)
    normed2 = gather_rows(normed2_f.astype(BF))
    active_f, swish_back = jax.vjp(
        lambda a, b: jax.nn.silu(a) * b, mm(normed2, w_gate), mm(normed2, w_up)
    )
    active = active_f.astype(BF)
    output = (valid_rows * (hidden + scatter_rows(mm(active, down_weight)))).astype(BF)
    grad_gate_f, grad_up_f = swish_back(mm_t(grad_branch, down_weight))
    grad_gate, grad_up = grad_gate_f.astype(BF), grad_up_f.astype(BF)
    grad_hidden_norm, grad_gain_two = norm_two_back(
        scatter_rows(mm_t(grad_gate, w_gate) + mm_t(grad_up, w_up))
    )
    grad_hidden = grad_result + grad_hidden_norm
    grad_mixed_in = gather_rows(grad_hidden.astype(BF))
    grad_mixed = mm_t(grad_mixed_in, output_weight).astype(BF)
    grad_mixed = grad_mixed.reshape(slot_len, kvs, per, head_width)
    probs_f = jnp.exp(scores_of() - log_total)
    grad_probs = jnp.einsum("rkgd,tkd->kgrt", grad_mixed, value, preferred_element_type=F32)
    grad_value = jnp.einsum(
        "kgrt,rkgd->tkd", probs_f.astype(BF), grad_mixed, preferred_element_type=F32
    )
    row_inner = jnp.sum(probs_f * grad_probs, axis=-1, keepdims=True)
    grad_scores = (probs_f * (grad_probs - row_inner)).astype(BF)
    grad_query = (
        jnp.einsum("kgrt,tkd->rkgd", grad_scores, key, preferred_element_type=F32) * score_scale
    )
    grad_key = (
        jnp.einsum("kgrt,rkgd->tkd", grad_scores, query, preferred_element_type=F32) * score_scale
    )
    grad_query_raw, grad_key_raw, grad_gain_query, grad_gain_key = turn_back(
        (grad_query.reshape(slot_len, heads, head_width), grad_key)
    )
    grad_query_b = grad_query_raw.reshape(slot_len, -1).astype(BF)
    grad_key_b = grad_key_raw.reshape(slot_len, -1).astype(BF)
    grad_value_b = grad_value.reshape(slot_len, -1).astype(BF)
    grad_normed = (
        mm_t(grad_query_b, w_qkv[0]) + mm_t(grad_key_b, w_qkv[1]) + mm_t(grad_value_b, w_qkv[2])
    )
    grad_inputs_norm, grad_gain_one = norm_one_back(scatter_rows(grad_normed))
    input_grad = grad_hidden + grad_inputs_norm

    def total(v):
        return lax.psum(v.astype(BF), "replica").astype(F32)

    grad_down = total(mm_w(active, grad_branch))
    grad_gate_w = to_rows(total(mm_w(normed2, grad_gate)).astype(BF)).astype(F32)
    grad_up_w = to_rows(total(mm_w(normed2, grad_up)).astype(BF)).astype(F32)
    grad_output_w = total(mm_w(mixed, grad_mixed_in))
    grad_query_w = to_rows(total(mm_w(normed, grad_query_b)).astype(BF)).astype(F32)
    grad_key_w = to_rows(total(mm_w(normed, grad_key_b)).astype(BF)).astype(F32)
    grad_value_w = to_rows(total(mm_w(normed, grad_value_b)).astype(BF)).astype(F32)
    small = jnp.concatenate([grad_gain_one, grad_gain_two, grad_gain_query, grad_gain_key])
    small = lax.psum(small, ("shard", "replica"))
    at = lax.axis_index("shard")
    hw = query_gain.shape[0]

    def own(start, size):
        return lax.dynamic_slice_in_dim(small, start + at * size, size)

    model = wide * shard_count
    return (
        output[None],
        input_grad[None],
        own(0, wide),
        grad_query_w,
        grad_key_w,
        grad_value_w,
        grad_output_w,
        own(2 * model, hw),
        own(2 * model + head_width, hw),
        own(model, wide),
        grad_gate_w,
        grad_up_w,
        grad_down,
    )


def solution(mesh):
    rows, mat, vec = P("replica", "shard", None), P("shard", None), P("shard")
    placed = (rows, rows, P("replica"), P("replica", None), vec, mat, mat, mat, mat)
    placed += (vec, vec, vec, mat, mat, mat)
    outs = (rows, rows, vec, mat, mat, mat, mat, vec, vec, vec, mat, mat, mat)
    return jax.shard_map(shards, mesh=mesh, in_specs=placed, out_specs=outs, check_vma=False)
```

time: 1540 us -> 769 us (0.50)
  waiting for transfers between devices: 1230 us -> 400 us
  blocking collectives: 48.1 us -> 120 us
  matrix products: 155 us -> 97.4 us
  starting transfers between devices: 1.23 us -> 29.9 us
  other arithmetic: 39.9 us -> 56.2 us
    reduce_scatter x9 -> x4, waiting for transfers between devices: 561 us -> 63.4 us  [scatter_rows(): lax.psum_scatter(v.astype(BF), 'shard', scatter_dimension=0, tiled=True)]
    all_gather x9 -> x4, waiting for transfers between devices: 213 us -> 11 us  [gather_rows(): return lax.all_gather(v, 'shard', axis=0, tiled=True)]
    psum x1, waiting for transfers between devices: 448 us -> 247 us  [total(): return lax.psum(v.astype(BF), 'replica').astype(F32)]
    all_to_all x0 -> x7, waiting for transfers between devices: none -> 78.6 us  [the longest x5 72.1 us: to_columns(): return lax.all_to_all(w, 'shard', split_axis=1, concat_axis=0, tiled=True)]
    dot_general x26 -> x27, matrix products: 151 us -> 97.4 us  [the longest x7 22 us: mm(): return jnp.einsum('ri,io->ro', a, b, preferred_element_type=F32)]
    all_to_all x0 -> x3, blocking collectives: none -> 49.4 us  [to_rows(): return lax.all_to_all(g, 'shard', split_axis=0, concat_axis=1, tiled=True)]
    psum x1, blocking collectives: 22.8 us -> 62.1 us  [shards(): small = lax.psum(small, ('shard', 'replica'))]
    all_to_all x0 -> x7, starting transfers between devices: none -> 28.7 us  [the longest x5 20.6 us: to_columns(): return lax.all_to_all(w, 'shard', split_axis=1, concat_axis=0, tiled=True)]
  transfers between devices with their start and end apart: 19 -> 16, of which waited for: 18 -> 10; matrix products, arithmetic and copies ran while one was open for 10% -> 11% of each run, Pallas kernels for 0% -> 0%
where the time goes in v1:
time: 769 us; the launch traced here: 765 us
  waiting for transfers between devices  400 us (52%)
  blocking collectives  120 us (16%)
  matrix products  97.4 us (13%)
  other arithmetic  56.2 us (7%)
  local copies, waits for them, and re-layouts  44.7 us (6%)
  starting transfers between devices  29.9 us (4%)
  between operations  16.3 us (2%)
    psum x1, waiting for transfers between devices, total(): return lax.psum(v.astype(BF), 'replica').astype(F32)  247 us
    all_to_all x5, waiting for transfers between devices, to_columns(): return lax.all_to_all(w, 'shard', split_axis=1, concat_axis=0, tiled=True)  72.1 us
    reduce_scatter x4, waiting for transfers between devices, scatter_rows(): lax.psum_scatter(v.astype(BF), 'shard', scatter_dimension=0, tiled=True)  63.4 us
    psum x1, blocking collectives, shards(): small = lax.psum(small, ('shard', 'replica'))  62.1 us
    all_to_all x3, blocking collectives, to_rows(): return lax.all_to_all(g, 'shard', split_axis=0, concat_axis=1, tiled=True)  49.4 us
    dot_general x7, matrix products, mm(): return jnp.einsum('ri,io->ro', a, b, preferred_element_type=F32)  22 us
    dot_general x7, matrix products, mm_t(): return jnp.einsum('ro,io->ri', a, b, preferred_element_type=F32)  21.9 us
    all_to_all x5, starting transfers between devices, to_columns(): return lax.all_to_all(w, 'shard', split_axis=1, concat_axis=0, tiled=True)  20.6 us
  transfers between devices with their start and end apart: 16, of which 10 were waited for; matrix products, arithmetic and copies ran while one was open for 11% of the time, Pallas kernels for 0%

profile of v1, /device:TPU:0, one launch (start us, length us, event | category | flops | bytes accessed | tf_op | source)
XLA Modules:
  0.0 764.7 jit_solution(12287463658765484522)
XLA Ops:
  11.5 8.5 %all-reduce.4 = bf16[2304]{0:T(1024)(128)(2,1)S(1)} all-reduce(bf16[2304]{0:T(1024)(128)(2,1)S(1)} %dynamic-update-slice.3), channel_id=2, replica_groups=mesh['shard'=4,'replica'=8] {'shard'}, use_global_device_ids=true, to_apply=%add.4 | all-reduce | flops 2304 | bytes 9216
  23.4 3.5 all-to-all-start.1
  28.5 4.6 compare_select_fusion.1
  33.1 6.2 all-to-all-done.1
  39.3 4.1 all-to-all-start
  47.2 5.5 all-to-all-done
  52.7 4.3 all-to-all-start.2
  57.3 2.9 broadcast_multiply_fusion.2
  64.9 6.6 all-to-all-done.2
  82.9 3.4 fusion.4
  86.3 3.7 exponential_reduce_fusion
  92.0 6.1 convolution_convert_fusion.8
  98.1 3.9 convolution_convert_fusion
  102.1 31.8 %reduce-scatter.5.cloned.1.call-done = bf16[256,1024]{1,0:T(8,128)(2,1)} async-done(((bf16[1024,1024]{1,0:T(8,128)(2,1)}), bf16[256,1024]{1,0:T(8,128)(2,1)}) %reduce-scatter.5.cloned.1.call-update) | async-done | bytes 524304 | tf_op jit(solution)/shard_map/reduce_scatter | solution.py:50
  137.3 2.6 copy.111
  139.8 4.3 all-to-all-start.3
  147.0 2.6 copy.113
  149.6 25.8 %all-to-all-done.3 = bf16[256,4,768]{0,2,1:T(8,128)(2,1)} async-done(((bf16[256,4,768]{0,2,1:T(8,128)(2,1)}), bf16[256,4,768]{0,2,1:T(8,128)(2,1)}, u32[]{:S(2)}, u32[]{:S(2)}) %all-to-all-start.3) | async-done | bytes 1572896 | tf_op jit(solution)/shard_map/all_to_all | solution.py:54
  175.4 4.4 all-to-all-start.4
  179.9 2.8 copy.112
  182.7 28.1 %all-to-all-done.4 = bf16[256,4,768]{0,2,1:T(8,128)(2,1)} async-done(((bf16[256,4,768]{0,2,1:T(8,128)(2,1)}), bf16[256,4,768]{0,2,1:T(8,128)(2,1)}, u32[]{:S(2)}, u32[]{:S(2)}) %all-to-all-start.4) | async-done | bytes 1572896 | tf_op jit(solution)/shard_map/all_to_all | solution.py:54
  213.4 5.6 fusion.63
  219.0 3.5 fusion.62
  222.5 7.2 multiply_convert_fusion
  232.3 3.1 add_convert_fusion.1
  235.5 31.5 %reduce-scatter.9.cloned.1.call-done = bf16[256,1024]{1,0:T(8,128)(2,1)} async-done(((bf16[1024,1024]{1,0:T(8,128)(2,1)}), bf16[256,1024]{1,0:T(8,128)(2,1)}) %reduce-scatter.9.cloned.1.call-update) | async-done | bytes 524304 | tf_op jit(solution)/shard_map/reduce_scatter | solution.py:50
  268.7 2.6 fusion.53
  271.8 5.2 convolution_convert_fusion.3
  277.0 3.1 convolution_convert_fusion.4
  280.1 3.0 convolution_convert_fusion.2
  283.1 11.0 %all-gather.12.cloned.1.call-done = bf16[1024,1024]{1,0:T(8,128)(2,1)} async-done(((bf16[256,1024]{1,0:T(8,128)(2,1)}), bf16[1024,1024]{1,0:T(8,128)(2,1)}) %all-gather.12.cloned.1.call-update) | async-done | bytes 2097168 | tf_op jit(solution)/shard_map/all_gather | solution.py:46
  294.1 3.1 convolution_convert_fusion.7
  297.2 8.5 %fusion.18 = bf16[2,128,1024]{2,1,0:T(8,128)(2,1)S(1)} fusion(bf16[1024,2,2,128]{0,3,2,1:T(8,128)(2,1)S(1)} %bitcast.261, f32[2,1024,1024,2]{2,1,3,0:T(8,128)} %copy-done.1, f32[2,2,1024]{2,1,0:T(2,128)S(1)} %log_add_fusion, pred[1024,1024]{0,1:T(8,128)(4,1)S(1)} %broadcast_compare_fusion), kind=kOutput, calls=%fused_computation.65 | convolution fusion | flops 1090781184 | bytes 19415040 | tf_op jit(solution)/shard_map/kgrt,rkgd->tkd/dot_general | solution.py:158
  305.8 12.4 %fusion = (f32[2,2,1024]{2,1,0:T(2,128)S(1)}, f32[2,1024,1024,2]{2,1,3,0:T(8,128)}) fusion(f32[2,1024,1024,2]{2,1,3,0:T(8,128)} %copy-done.1, f32[2,2,1024]{2,1,0:T(2,128)S(1)} %log_add_fusion, pred[1024,1024]{0,1:T(8,128)(4,1)S(1)} %broadcast_compare_fusion, bf16[1024,2,128,1]{0,2,3,1:T(8,128)(2,1)S(1)} %bitcast.264, bf16[1024,2,2,128]{0,3,2,1:T(8,128)(2,1)S(1)} %bitcast.262), kind=kOutput, calls=%fused_computation.2 | convolution fusion | flops 1094709248 | bytes 36208640 | tf_op jit(solution)/shard_map/rkgd,tkd->kgrt/dot_general | solution.py:157
  318.2 12.4 %fusion.2 = bf16[2,2,1024,1024]{2,3,1,0:T(8,128)(2,1)S(1)} fusion(f32[2,1024,1024,2]{2,1,3,0:T(8,128)} %get-tuple-element.84, f32[2,1024,1024,2]{2,1,3,0:T(8,128)} %copy-done.1, f32[2,2,1024]{2,1,0:T(2,128)S(1)} %get-tuple-element.83, f32[2,2,1024]{2,1,0:T(2,128)S(1)} %log_add_fusion, pred[1024,1024]{0,1:T(8,128)(4,1)S(1)} %broadcast_compare_fusion), kind=kLoop, calls=%fused_computation.4 | loop fusion | flops 25165824 | bytes 43024384 | tf_op jit(solution)/shard_map/convert_element_type | solution.py:162
  332.0 2.9 broadcast_multiply_fusion
  354.6 3.9 add_convert_fusion
  358.5 4.5 convolution_convert_fusion.1
  363.1 247.1 %all-reduce.8.cloned.1.call-done = (bf16[4,256,512]{2,1,0:T(8,128)(2,1)}, bf16[4,256,256]{2,1,0:T(8,128)(2,1)}, bf16[4,256,256]{2,1,0:T(8,128)(2,1)}, bf16[512,1...) async-done(((bf16[4,256,512]{2,1,0:T(8,128)(2,1)}, bf16[4,256,256]{2,1,0:T(8,128)(2,1)}, ...) | async-done | bytes 7864336 | tf_op jit(solution)/shard_map/psum | solution.py:182
  610.2 13.2 %all_to_all.160 = bf16[4,256,256]{2,1,0:T(8,128)(2,1)} all-to-all(bf16[4,256,256]{2,1,0:T(8,128)(2,1)} %get-tuple-element.34), channel_id=1, replica_groups=mesh['shard'=4,'replica'=8] {'shard'}, dimensions={0} | all-to-all | bytes 1048576 | tf_op jit(solution)/shard_map/all_to_all | solution.py:58
  623.4 18.6 %all_to_all.161 = bf16[4,256,256]{2,1,0:T(8,128)(2,1)} all-to-all(bf16[4,256,256]{2,1,0:T(8,128)(2,1)} %get-tuple-element.35), channel_id=1, replica_groups=mesh['shard'=4,'replica'=8] {'shard'}, dimensions={0} | all-to-all | bytes 1048576 | tf_op jit(solution)/shard_map/all_to_all | solution.py:58
  642.0 17.6 %all_to_all.162 = bf16[4,256,512]{2,1,0:T(8,128)(2,1)} all-to-all(bf16[4,256,512]{2,1,0:T(8,128)(2,1)S(1)} %copy-done.34), channel_id=1, replica_groups=mesh['shard'=4,'replica'=8] {'shard'}, dimensions={0} | all-to-all | bytes 2097152 | tf_op jit(solution)/shard_map/all_to_all | solution.py:58
  659.6 4.5 all-to-all-start.9
  665.7 62.1 %psum.56 = f32[2304]{0:T(1024)S(1)} all-reduce(f32[2304]{0:T(1024)S(1)} %pad_maximum_fusion.1), channel_id=1, replica_groups=mesh['shard'=4,'replica'=8] {'shard','replica'}, use_global_device_ids=true, to_apply=%region_19.20 | all-reduce | flops 2304 | bytes 18432 | tf_op jit(solution)/shard_map/psum | solution.py:192
  728.5 3.4 fusion.30
  731.9 3.6 all-to-all-start.8
  736.0 2.8 convert_element_type.304
  749.1 6.4 all-to-all-done.8
  (215 shorter events, 79.9 us)
Async XLA Ops:
  7.2 215.3 %copy-start = (bf16[768,1024]{1,0:T(8,128)(2,1)S(1)}, bf16[768,1024]{1,0:T(8,128)(2,1)}, u32[]{:S(2)}) copy-start(bf16[768,1024]{1,0:T(8,128)(2,1)} %param.31) | copy-start | bytes 4718596
  7.2 15.0 %copy-start.39 = (bf16[256,1024]{1,0:T(8,128)(2,1)S(1)}, bf16[256,1024]{1,0:T(8,128)(2,1)}, u32[]{:S(2)}) copy-start(bf16[256,1024]{1,0:T(8,128)(2,1)} %param.23) | copy-start | bytes 1572868
  7.2 66.6 %all-gather.6.cloned.1.call-start = ((), (), s32[]{:S(2)}) async-start(), calls=%async_computation.14 | async-start | bytes 2621440 | tf_op jit(solution)/shard_map/all_gather | solution.py:46
  22.2 4.8 copy-start.40
  22.2 5.7 copy-start.41
  23.4 15.9 %all-to-all-start.1 = ((bf16[256,4,256]{2,0,1:T(8,128)(2,1)}), bf16[256,4,256]{2,0,1:T(8,128)(2,1)S(1)}, u32[]{:S(2)}, u32[]{:S(2)}) async-start(bf16[256,4,256]{2,0,1:T(8,128)(2,1)} %copy.103), calls=%async_computation.1 | async-start | bytes 1048576 | tf_op jit(solution)/shard_map/all_to_all | solution.py:54
  39.3 7.2 copy-start.13
  39.3 13.4 %all-to-all-start = ((bf16[256,4,256]{0,2,1:T(8,128)(2,1)}), bf16[256,4,256]{0,2,1:T(8,128)(2,1)}, u32[]{:S(2)}, u32[]{:S(2)}) async-start(bf16[256,4,256]{0,2,1:T(8,128)(2,1)} %bitcast.17), calls=%async_computation | async-start | bytes 1048576 | tf_op jit(solution)/shard_map/all_to_all | solution.py:54
  52.7 18.8 %all-to-all-start.2 = ((bf16[256,4,512]{2,0,1:T(8,128)(2,1)}), bf16[256,4,512]{2,0,1:T(8,128)(2,1)}, u32[]{:S(2)}, u32[]{:S(2)}) async-start(bf16[256,4,512]{2,0,1:T(8,128)(2,1)} %copy.106), calls=%async_computation.2 | async-start | bytes 2097152 | tf_op jit(solution)/shard_map/all_to_all | solution.py:54
  57.0 76.9 %reduce-scatter.5.cloned.1.call-start = ((), (), s32[]{:S(2)}) async-start(), calls=%async_computation.15 | async-start | bytes 2621440 | tf_op jit(solution)/shard_map/reduce_scatter | solution.py:50
  60.2 21.9 %copy-start.8 = (f32[1024,128]{0,1:T(8,128)}, f32[1024,128]{0,1:T(8,128)S(1)}, u32[]{:S(2)}) copy-start(f32[1024,128]{0,1:T(8,128)S(1)} %get-tuple-element.60) | copy-start | bytes 1572868
  76.2 4.3 copy-start.5
  76.2 2.3 copy-start.42
  82.8 3.4 copy-start.16
  86.3 5.8 copy-start.1
  86.3 3.7 copy-start.21
  90.8 7.3 copy-start.36
  92.0 6.1 copy-start.48
  102.0 31.9 %copy-start.4 = (bf16[1,256,1024]{2,1,0:T(8,128)(2,1)S(1)}, bf16[1,256,1024]{2,1,0:T(8,128)(2,1)}, u32[]{:S(2)}) copy-start(bf16[1,256,1024]{2,1,0:T(8,128)(2,1)} %param.17) | copy-start | bytes 1572868
  102.0 111.4 %all-gather.8.cloned.1.call-start = ((), (), s32[]{:S(2)}) async-start(), calls=%async_computation.16 | async-start | bytes 2621440 | tf_op jit(solution)/shard_map/all_gather | solution.py:46
  139.8 35.6 %all-to-all-start.3 = ((bf16[256,4,768]{0,2,1:T(8,128)(2,1)}), bf16[256,4,768]{0,2,1:T(8,128)(2,1)}, u32[]{:S(2)}, u32[]{:S(2)}) async-start(bf16[256,4,768]{0,2,1:T(8,128)(2,1)} %bitcast.234), calls=%async_computation.4 | async-start | bytes 3145728 | tf_op jit(solution)/shard_map/all_to_all | solution.py:54
  144.2 78.3 %all-gather.10.cloned.1.call-start = ((), (), s32[]{:S(2)}) async-start(), calls=%async_computation.18 | async-start | bytes 2621440 | tf_op jit(solution)/shard_map/all_gather | solution.py:46
  175.4 35.4 %all-to-all-start.4 = ((bf16[256,4,768]{0,2,1:T(8,128)(2,1)}), bf16[256,4,768]{0,2,1:T(8,128)(2,1)}, u32[]{:S(2)}, u32[]{:S(2)}) async-start(bf16[256,4,768]{0,2,1:T(8,128)(2,1)} %bitcast.235), calls=%async_computation.5 | async-start | bytes 3145728 | tf_op jit(solution)/shard_map/all_to_all | solution.py:54
  179.8 87.2 %reduce-scatter.9.cloned.1.call-start = ((), (), s32[]{:S(2)}) async-start(), calls=%async_computation.19 | async-start | bytes 2621440 | tf_op jit(solution)/shard_map/reduce_scatter | solution.py:50
  213.4 5.6 copy-start.30
  213.4 5.7 copy-start.44
  222.5 7.2 copy-start.31
  229.7 2.5 copy-start.32
  235.4 58.6 %all-gather.12.cloned.1.call-start = ((), (), s32[]{:S(2)}) async-start(), calls=%async_computation.20 | async-start | bytes 2621440 | tf_op jit(solution)/shard_map/all_gather | solution.py:46
  271.3 338.9 %all-reduce.8.cloned.1.call-start = ((), (), s32[]{:S(2)}) async-start(), calls=%async_computation.22 | async-start | bytes 15728640 | tf_op jit(solution)/shard_map/psum | solution.py:182
  271.8 5.2 copy-start.45
  271.8 5.2 copy-start.52
  277.0 3.1 copy-start.47
  277.0 3.1 copy-start.53
  297.2 8.5 %copy-start.37 = (bf16[1024,256]{0,1:T(8,128)(2,1)S(1)}, bf16[1024,256]{0,1:T(8,128)(2,1)}, u32[]{:S(2)}) copy-start(bf16[1024,256]{0,1:T(8,128)(2,1)} %copy-done.36) | copy-start | bytes 1572868
  305.8 39.2 %copy-start.38 = (bf16[2,128,1024]{2,1,0:T(8,128)(2,1)}, bf16[2,128,1024]{2,1,0:T(8,128)(2,1)S(1)}, u32[]{:S(2)}) copy-start(bf16[2,128,1024]{2,1,0:T(8,128)(2,1)S(1)} %fusion.18) | copy-start | bytes 1572868
  318.2 12.4 %copy-start.29 = (bf16[1024,2,128,1]{0,2,3,1:T(8,128)(2,1)S(1)}, bf16[1024,2,128,1]{0,2,3,1:T(8,128)(2,1)}, u32[]{:S(2)}) copy-start(bf16[1024,2,128,1]{0,2,3,1:T(8,128)(2,1)} %copy-done.28) | copy-start | bytes 1572868
  340.6 5.9 copy-start.25
  342.7 5.4 copy-start.19
  350.4 2.9 copy-start.14
  350.4 313.7 %reduce-scatter.11.cloned.1.call-start = ((), (), s32[]{:S(2)}) async-start(), calls=%async_computation.21 | async-start | bytes 2621440 | tf_op jit(solution)/shard_map/reduce_scatter | solution.py:50
  358.5 370.0 %reduce-scatter.7.cloned.1.call-start = ((), (), s32[]{:S(2)}) async-start(), calls=%async_computation.17 | async-start | bytes 2621440 | tf_op jit(solution)/shard_map/reduce_scatter | solution.py:50
  610.2 31.7 %copy-start.34 = (bf16[4,256,512]{2,1,0:T(8,128)(2,1)S(1)}, bf16[4,256,512]{2,1,0:T(8,128)(2,1)}, u32[]{:S(2)}) copy-start(bf16[4,256,512]{2,1,0:T(8,128)(2,1)} %get-tuple-element.33) | copy-start | bytes 3145732
  659.6 68.9 %copy-start.7 = (bf16[256,1024]{1,0:T(8,128)(2,1)S(1)}, bf16[256,1024]{1,0:T(8,128)(2,1)}, u32[]{:S(2)}) copy-start(bf16[256,1024]{1,0:T(8,128)(2,1)} %reduce-scatter.5.cloned.1.call-done) | copy-start | bytes 1572868
  659.6 68.9 %copy-start.12 = (bf16[1,256,1024]{2,1,0:T(8,128)(2,1)S(1)}, bf16[1,256,1024]{2,1,0:T(8,128)(2,1)}, u32[]{:S(2)}) copy-start(bf16[1,256,1024]{2,1,0:T(8,128)(2,1)} %param.18) | copy-start | bytes 1572868
  659.6 72.2 %all-to-all-start.9 = ((bf16[4,256,768]{2,1,0:T(8,128)(2,1)}), bf16[4,256,768]{2,1,0:T(8,128)(2,1)}, u32[]{:S(2)}, u32[]{:S(2)}) async-start(bf16[4,256,768]{2,1,0:T(8,128)(2,1)} %get-tuple-element.38), calls=%async_computation.13 | async-start | bytes 3145728 | tf_op jit(solution)/shard_map/all_to_all | solution.py:58
  731.9 23.7 %all-to-all-start.8 = ((bf16[4,256,768]{2,1,0:T(8,128)(2,1)}), bf16[4,256,768]{2,1,0:T(8,128)(2,1)S(1)}, u32[]{:S(2)}, u32[]{:S(2)}) async-start(bf16[4,256,768]{2,1,0:T(8,128)(2,1)} %get-tuple-element.37), calls=%async_computation.12 | async-start | bytes 3145728 | tf_op jit(solution)/shard_map/all_to_all | solution.py:58
  735.4 3.4 copy-start.33
  (22 other events, 34.1 us)
Sparse Core Ops, SparseCore 0:
  22.3 26.2 all-gather.5
  102.1 31.7 reduce-scatter.4
  137.4 33.7 all-gather.7
  172.7 33.7 all-gather.9
  235.6 31.4 reduce-scatter.8
  271.5 22.5 all-gather.11
  350.6 259.6 all-reduce.7
  613.3 35.3 reduce-scatter.10
  652.0 42.2 reduce-scatter.6

commit v2 on v1

--- a/solution.py
+++ b/solution.py
@@ -1,12 +1,243 @@
 import jax
 import jax.numpy as jnp
 from jax import lax
+from jax.experimental import pallas as pl
+from jax.experimental.pallas import tpu as pltpu
 from jax.sharding import PartitionSpec as P
 
 EPSILON = 1e-06
 ROPE_BASE = 1000000.0
 BF = jnp.bfloat16
 F32 = jnp.float32
+
+
+class Topo:
+    def __init__(self, shards, replicas):
+        self.S=shards; self.R=replicas; self.L=replicas//2
+        self.s=lax.axis_index("shard"); r=lax.axis_index("replica")
+        self.r=r
+        L=self.L
+        self.a=lax.div(r,2); self.b=lax.rem(r,2)
+        self.m0=L//2-1; self.m1=L//2
+        a=self.a
+        self.left=a<=self.m0
+        self.mid=jnp.logical_or(a==self.m0,a==self.m1)
+        self.edge=jnp.logical_or(a==0,a==L-1)
+        self.toward=jnp.where(self.left,r+2,r-2)
+        self.outward=jnp.where(self.left,r-2,r+2)
+        self.h=jnp.where(self.left,0,1)
+    def rep(self, r): return (self.s, r)
+    def sh(self, k): return (self.s^k, self.r)
+
+def barrier(tp):
+    bar=pltpu.get_barrier_semaphore()
+    R=tp.R
+    ids=[tp.rep(tp.r^1), tp.rep(lax.rem(tp.r+2,R)), tp.rep(lax.rem(tp.r+R-2,R)), tp.sh(1), tp.sh(2), tp.sh(3)]
+    for d in ids:
+        pl.semaphore_signal(bar, inc=1, device_id=d, device_id_type=pl.DeviceIdType.MESH)
+    pl.semaphore_wait(bar, len(ids))
+
+def add_into(dst, a, b, blocks, rows, step):
+    def body(i, _):
+        q=pl.multiple_of(i*step, step)
+        for t in range(blocks):
+            dst[t, pl.ds(q,step), :] = (a[t, pl.ds(q,step), :].astype(F32)+b[t, pl.ds(q,step), :].astype(F32)).astype(BF)
+        return 0
+    lax.fori_loop(0, rows//step, body, 0)
+
+class Chunk:
+    def __init__(self, tp, kind, G, out, j, nr, spread, bufs, sems):
+        self.tp=tp; self.kind=kind; self.G=G; self.out=out; self.base=j*nr; self.nr=nr; self.hr=nr//2
+        self.spread=spread; self.bufs=bufs; self.sem_send, self.sem_recv, self.i=sems
+        self.W=G.shape[2]; self.W0=self.W
+        self.sent=[]
+        self.steps=self.steps_a() if kind=="A" else self.steps_b()
+    def half(self, h):
+        return self.G.at[:, pl.ds(pl.multiple_of(self.base+h*self.hr,16), self.hr), :]
+    def full(self):
+        return self.G.at[:, pl.ds(self.base, self.nr), :]
+    def out_half(self, h):
+        rows=pl.ds(pl.multiple_of(self.base+h*self.hr,16), self.hr)
+        return self.out.at[rows, :] if self.spread else self.out.at[:, rows, :]
+    def out_piece(self, h, s):
+        rows=pl.ds(pl.multiple_of(self.base+h*self.hr,16), self.hr)
+        return self.out.at[rows, pl.ds(pl.multiple_of(s*self.W,128), self.W)]
+    def copy(self, slot, src, dst, dev):
+        return pltpu.make_async_remote_copy(src, dst, self.sem_send.at[self.i*10+slot], self.sem_recv.at[self.i*10+slot], device_id=dev, device_id_type=pl.DeviceIdType.MESH)
+    def start(self, cond, slot, src, dst, dev):
+        c=self.copy(slot,src,dst,dev)
+        if cond is None:
+            c.start()
+        else:
+            pl.when(cond)(lambda: c.start())
+        self.sent.append((cond,c))
+    def drain(self):
+        for cond,c in self.sent:
+            if cond is None: c.wait_send()
+            else: pl.when(cond)(lambda c=c: c.wait_send())
+    def recv(self, slot, ref):
+        self.copy(slot, ref, ref, self.tp.rep(self.tp.r^1)).wait_recv()
+    def final_out(self, h, F):
+        tp=self.tp
+        if self.spread:
+            for k in (1,2,3):
+                blk=tp.s^k
+                self.start(tp.mid, 2+k, F.at[blk], self.out_piece(h, tp.s), tp.sh(k))
+        @pl.when(tp.mid)
+        def _():
+            if self.spread:
+                pltpu.make_async_copy(F.at[tp.s], self.out_piece(h, tp.s), self.sem_send.at[self.i*10+9]).start()
+            else:
+                pltpu.make_async_copy(F, self.out_half(h), self.sem_send.at[self.i*10+9]).start()
+    def final_wait(self, h, F):
+        tp=self.tp
+        if self.spread:
+            for k in (1,2,3):
+                self.copy(2+k, F.at[0], self.out_piece(h, tp.s^k), tp.sh(k)).wait_recv()
+            pltpu.make_async_copy(F.at[tp.s], self.out_piece(h, tp.s), self.sem_send.at[self.i*10+9]).wait()
+        else:
+            pltpu.make_async_copy(F, self.out_half(h), self.sem_send.at[self.i*10+9]).wait()
+    def steps_a(self):
+        tp=self.tp; b=tp.b; RX,FOLD,MID=self.bufs; xp=tp.rep(tp.r^1)
+        not_edge=jnp.logical_not(tp.edge); not_mid=jnp.logical_not(tp.mid)
+        has_outer=not_edge
+        own=self.half(b)
+        def push(cond):
+            self.start(jnp.logical_and(cond,tp.mid), 2, own, MID, tp.rep(tp.toward))
+            if tp.L>2: self.start(jnp.logical_and(cond,not_mid), 1, own, FOLD, tp.rep(tp.toward))
+        def s0():
+            self.start(None, 0, self.half(1-b), RX, xp)
+        def s1():
+            self.recv(0,RX)
+            add_into(own, own, RX, 4, self.hr, 16)
+            push(tp.edge)
+        def s2():
+            if tp.L==2: return
+            @pl.when(has_outer)
+            def _():
+                self.recv(1,FOLD)
+                add_into(own, own, FOLD, 4, self.hr, 16)
+            push(has_outer)
+        def s3():
+            @pl.when(tp.mid)
+            def _():
+                self.recv(2,MID)
+                add_into(MID, own, MID, 4, self.hr, 16)
+            self.final_out(b, MID)
+        def s4():
+            @pl.when(tp.mid)
+            def _():
+                self.final_wait(b, MID)
+            if tp.L>2: self.start(tp.mid, 6, self.out_half(b), self.out_half(b), tp.rep(tp.outward))
+            self.start(tp.mid, 7, self.out_half(b), self.out_half(b), xp)
+        def s5():
+            if tp.L==2: return
+            @pl.when(not_mid)
+            def _():
+                self.recv(6,self.out_half(b))
+            if tp.L>4: self.start(jnp.logical_and(not_mid,not_edge), 6, self.out_half(b), self.out_half(b), tp.rep(tp.outward))
+            self.start(not_mid, 7, self.out_half(b), self.out_half(b), xp)
+        def s6():
+            self.recv(7,self.out_half(1-b))
+        return [s0,s1,s2,s3,s4,s5,s6]
+    def steps_b(self):
+        tp=self.tp; h=tp.h; FOLD,MID,XB=self.bufs; xp=tp.rep(tp.r^1)
+        not_edge=jnp.logical_not(tp.edge); not_mid=jnp.logical_not(tp.mid)
+        own=self.half(h); full=self.full()
+        def push(cond):
+            self.start(jnp.logical_and(cond,tp.mid), 2, self.half(1-h), MID, tp.rep(tp.toward))
+            if tp.L>2: self.start(jnp.logical_and(cond,not_mid), 1, full, FOLD, tp.rep(tp.toward))
+        def s0():
+            push(tp.edge)
+        def s1():
+            if tp.L==2: return
+            @pl.when(not_edge)
+            def _():
+                self.recv(1,FOLD)
+                add_into(full, full, FOLD, 4, self.nr, 16)
+            push(not_edge)
+        def s2():
+            @pl.when(tp.mid)
+            def _():
+                self.recv(2,MID)
+                add_into(own, own, MID, 4, self.hr, 16)
+            self.start(tp.mid, 0, own, XB, xp)
+        def s3():
+            @pl.when(tp.mid)
+            def _():
+                self.recv(0,XB)
+                add_into(XB, own, XB, 4, self.hr, 16)
+            self.final_out(h, XB)
+        def s4():
+            @pl.when(tp.mid)
+            def _():
+                self.final_wait(h, XB)
+            self.start(tp.mid, 8, self.out_half(h), self.out_half(h), tp.rep(tp.toward))
+            if tp.L>2: self.start(tp.mid, 6, self.out_half(h), self.out_half(h), tp.rep(tp.outward))
+        def s5():
+            @pl.when(tp.mid)
+            def _():
+                self.recv(8,self.out_half(1-h))
+            if tp.L==2: return
+            self.start(tp.mid, 7, self.out_half(1-h), self.out_half(1-h), tp.rep(tp.outward))
+            @pl.when(not_mid)
+            def _():
+                self.recv(6,self.out_half(h))
+            if tp.L>4: self.start(jnp.logical_and(not_mid,not_edge), 6, self.out_half(h), self.out_half(h), tp.rep(tp.outward))
+        def s6():
+            if tp.L==2: return
+            @pl.when(not_mid)
+            def _():
+                self.recv(7,self.out_half(1-h))
+            if tp.L>4: self.start(jnp.logical_and(not_mid,not_edge), 7, self.out_half(1-h), self.out_half(1-h), tp.rep(tp.outward))
+        return [s0,s1,s2,s3,s4,s5,s6]
+
+ARR=dict(gu=(256,1536,True,64), d=(192,1024,False,64), o=(128,1024,False,64), qkv=(256,1024,True,32))
+ORDER=["d","gu","o","qkv"]
+
+def plan():
+    chunks=[]; i=0
+    for n in ORDER:
+        rows,W,sp,nr=ARR[n]
+        for j in range(rows//nr):
+            chunks.append((n,j,"A" if i%2==0 else "B")); i+=1
+    return chunks
+
+def scratch(chunks):
+    scr=[]
+    for n,j,k in chunks:
+        rows,W,sp,nr=ARR[n]
+        h=pltpu.VMEM((4,nr//2,W),BF); f=pltpu.VMEM((4,nr,W),BF)
+        scr += [h,h,h] if k=="A" else [f,h,h]
+    n=len(chunks)
+    return scr+[pltpu.SemaphoreType.DMA((n*10,)),pltpu.SemaphoreType.DMA((n*10,))]
+
+def make(S,R):
+    chunks=plan(); nb=3*len(chunks)
+    def kern(*refs):
+        ins=dict(zip(ORDER,refs[:4])); outs=dict(zip(ORDER,refs[4:8]));
+        G=dict(zip(ORDER,refs[8:12])); ld=refs[12]
+        bufs=refs[13:13+nb]; send,recv=refs[13+nb:]
+        tp=Topo(S,R)
+        for i,n in enumerate(ORDER):
+            pltpu.make_async_copy(ins[n],G[n],ld.at[i]).start()
+        barrier(tp)
+        for i,n in enumerate(ORDER):
+            pltpu.make_async_copy(ins[n],G[n],ld.at[i]).wait()
+        cs=[Chunk(tp,k,G[n],outs[n],j,ARR[n][3],ARR[n][2],bufs[3*i:3*i+3],(send,recv,i)) for i,(n,j,k) in enumerate(chunks)]
+        ns=7
+        for t in range(len(cs)+ns-1):
+            for st in range(ns-1,-1,-1):
+                i=t-st
+                if 0<=i<len(cs): cs[i].steps[st]()
+        for c in cs: c.drain()
+    out_shape=[jax.ShapeDtypeStruct((ARR[n][0],4*ARR[n][1]) if ARR[n][2] else (4,ARR[n][0],ARR[n][1]),BF) for n in ORDER]
+    any_=pl.BlockSpec(memory_space=pl.ANY)
+    def call(*gs):
+        return pl.pallas_call(kern,out_shape=out_shape,in_specs=[any_]*4,out_specs=[any_]*4,
+            scratch_shapes=[pltpu.VMEM((4,ARR[n][0],ARR[n][1]),BF) for n in ORDER]+[pltpu.SemaphoreType.DMA((4,))]+scratch(chunks),
+            compiler_params=pltpu.CompilerParams(collective_id=1,has_side_effects=True,vmem_limit_bytes=60<<20),name="grad_sum")(*gs)
+    return call
 
 
 def rms_scale(values, gain_vec):
@@ -178,16 +409,30 @@
     grad_inputs_norm, grad_gain_one = norm_one_back(scatter_rows(grad_normed))
     input_grad = grad_hidden + grad_inputs_norm
 
-    def total(v):
-        return lax.psum(v.astype(BF), "replica").astype(F32)
-
-    grad_down = total(mm_w(active, grad_branch))
-    grad_gate_w = to_rows(total(mm_w(normed2, grad_gate)).astype(BF)).astype(F32)
-    grad_up_w = to_rows(total(mm_w(normed2, grad_up)).astype(BF)).astype(F32)
-    grad_output_w = total(mm_w(mixed, grad_mixed_in))
-    grad_query_w = to_rows(total(mm_w(normed, grad_query_b)).astype(BF)).astype(F32)
-    grad_key_w = to_rows(total(mm_w(normed, grad_key_b)).astype(BF)).astype(F32)
-    grad_value_w = to_rows(total(mm_w(normed, grad_value_b)).astype(BF)).astype(F32)
+    def part(left, right):
+        g = mm_w(left, right).astype(BF)
+        return g.reshape(shard_count, g.shape[0] // shard_count, g.shape[1])
+
+    share = {
+        "d": part(active, grad_branch),
+        "gu": part(normed2, jnp.concatenate([grad_gate, grad_up], axis=1)),
+        "o": part(mixed, grad_mixed_in),
+        "qkv": part(normed, jnp.concatenate([grad_query_b, grad_key_b, grad_value_b], axis=1)),
+    }
+    sums = dict(zip(ORDER, make(shard_count, lax.axis_size("replica"))(*[share[n] for n in ORDER])))
+    grad_down = sums["d"].astype(F32).reshape(-1, sums["d"].shape[-1])
+    grad_output_w = sums["o"].astype(F32).reshape(-1, sums["o"].shape[-1])
+
+    def columns(v, start, width):
+        v = v.reshape(v.shape[0], shard_count, -1)[:, :, start : start + width]
+        return v.reshape(v.shape[0], -1).astype(F32)
+
+    fw, qw, kw = w_gate.shape[1], w_qkv[0].shape[1], w_qkv[1].shape[1]
+    grad_gate_w = columns(sums["gu"], 0, fw)
+    grad_up_w = columns(sums["gu"], fw, fw)
+    grad_query_w = columns(sums["qkv"], 0, qw)
+    grad_key_w = columns(sums["qkv"], qw, kw)
+    grad_value_w = columns(sums["qkv"], qw + kw, kw)
     small = jnp.concatenate([grad_gain_one, grad_gain_two, grad_gain_query, grad_gain_key])
     small = lax.psum(small, ("shard", "replica"))
     at = lax.axis_index("shard")

time: 769 us -> 675 us (0.88)
  waiting for transfers between devices: 400 us -> 158 us
  Pallas kernels: 0 us -> 213 us
  blocking collectives: 120 us -> 48 us
  local copies, waits for them, and re-layouts: 44.7 us -> 55.9 us
  starting transfers between devices: 29.9 us -> 21.4 us
    psum x1 -> x0, waiting for transfers between devices: 247 us -> none  [total(): return lax.psum(v.astype(BF), 'replica').astype(F32)]
    pallas_call x0 -> x1, Pallas kernels: none -> 213 us  [call(): pl.pallas_call(kern, out_shape=out_shape, in_specs=[any_] * 4, out_specs=...]
    all_to_all x3 -> x0, blocking collectives: 49.4 us -> none  [to_rows(): return lax.all_to_all(g, 'shard', split_axis=0, concat_axis=1, tiled=True)]
    psum x1, blocking collectives: 62.1 us -> 39.5 us  [shards(): small = lax.psum(small, ('shard', 'replica'))]
    reshape x0 -> x2, local copies, waits for them, and re-layouts: none -> 12.1 us  [columns(): v = v.reshape(v.shape[0], shard_count, -1)[:, :, start:start + width]]
    all_gather x4, waiting for transfers between devices: 11 us -> 22.7 us  [gather_rows(): return lax.all_gather(v, 'shard', axis=0, tiled=True)]
    all_to_all x2 -> x0, starting transfers between devices: 8.1 us -> none  [to_rows(): return lax.all_to_all(g, 'shard', split_axis=0, concat_axis=1, tiled=True)]
    convert_element_type x5 -> x0, local copies, waits for them, and re-layouts: 7.93 us -> none  [the longest x1 2.09 us: shards(): to_rows(total(mm_w(normed2, grad_gate)).astype(BF)).astype(F32)]
  transfers between devices with their start and end apart: 16 -> 13, of which waited for: 10 -> 8; matrix products, arithmetic and copies ran while one was open for 11% -> 15% of each run, Pallas kernels for 0% -> 32%
where the time goes in v2:
time: 675 us; the launch traced here: 665 us
  Pallas kernels  213 us (32%)
  waiting for transfers between devices  158 us (23%)
  matrix products  94.5 us (14%)
  other arithmetic  57.5 us (9%)
  local copies, waits for them, and re-layouts  55.9 us (8%)
  blocking collectives  48 us (7%)
  starting transfers between devices  21.4 us (3%)
  between operations  16.5 us (2%)
    pallas_call x1, Pallas kernels, call(): pl.pallas_call(kern, out_shape=out_shape, in_specs=[any_] * 4, out_specs=...  213 us
    all_to_all x5, waiting for transfers between devices, to_columns(): return lax.all_to_all(w, 'shard', split_axis=1, concat_axis=0, tiled=True)  71.8 us
    reduce_scatter x4, waiting for transfers between devices, scatter_rows(): lax.psum_scatter(v.astype(BF), 'shard', scatter_dimension=0, tiled=True)  63.4 us
    psum x1, blocking collectives, shards(): small = lax.psum(small, ('shard', 'replica'))  39.5 us
    unnamed x127, local copies, waits for them, and re-layouts  27.6 us
    all_gather x4, waiting for transfers between devices, gather_rows(): return lax.all_gather(v, 'shard', axis=0, tiled=True)  22.7 us
    dot_general x7, matrix products, mm(): return jnp.einsum('ri,io->ro', a, b, preferred_element_type=F32)  22.2 us
    all_to_all x5, starting transfers between devices, to_columns(): return lax.all_to_all(w, 'shard', split_axis=1, concat_axis=0, tiled=True)  20.5 us
  transfers between devices with their start and end apart: 13, of which 8 were waited for; matrix products, arithmetic and copies ran while one was open for 15% of the time, Pallas kernels for 32%

profile of v2, /device:TPU:0, one launch (start us, length us, event | category | flops | bytes accessed | tf_op | source)
XLA Modules:
  0.0 665.4 jit_solution(14443025746600508577)
XLA Ops:
  11.6 8.5 %all-reduce.4 = bf16[2304]{0:T(1024)(128)(2,1)S(1)} all-reduce(bf16[2304]{0:T(1024)(128)(2,1)S(1)} %dynamic-update-slice.3), channel_id=2, replica_groups=mesh['shard'=4,'replica'=8] {'shard'}, use_global_device_ids=true, to_apply=%add.4 | all-reduce | flops 2304 | bytes 9216
  23.5 3.5 all-to-all-start.1
  28.6 4.6 compare_select_fusion.1
  33.2 6.2 all-to-all-done.1
  39.4 4.1 all-to-all-start
  47.3 5.5 all-to-all-done
  52.7 4.2 all-to-all-start.2
  57.7 2.8 broadcast_multiply_fusion.2
  65.3 6.2 all-to-all-done.2
  71.5 2.3 copy.87
  73.8 2.4 multiply_reduce_fusion.6
  82.9 3.4 fusion.4
  86.3 3.7 exponential_reduce_fusion
  92.0 6.1 convolution_convert_fusion.6
  98.1 3.9 convolution_convert_fusion.1
  102.1 31.8 %reduce-scatter.5.cloned.1.call-done = bf16[256,1024]{1,0:T(8,128)(2,1)} async-done(((bf16[1024,1024]{1,0:T(8,128)(2,1)}), bf16[256,1024]{1,0:T(8,128)(2,1)}) %reduce-scatter.5.cloned.1.call-update) | async-done | bytes 524304 | tf_op jit(solution)/shard_map/reduce_scatter | solution.py:281
  137.3 2.6 copy.91
  139.8 4.3 all-to-all-start.3
  147.0 2.6 copy.93
  149.6 25.8 %all-to-all-done.3 = bf16[256,4,768]{0,2,1:T(8,128)(2,1)} async-done(((bf16[256,4,768]{0,2,1:T(8,128)(2,1)}), bf16[256,4,768]{0,2,1:T(8,128)(2,1)}, u32[]{:S(2)}, u32[]{:S(2)}) %all-to-all-start.3) | async-done | bytes 1572896 | tf_op jit(solution)/shard_map/all_to_all | solution.py:285
  175.4 4.3 all-to-all-start.4
  179.8 2.8 copy.92
  182.7 28.1 %all-to-all-done.4 = bf16[256,4,768]{0,2,1:T(8,128)(2,1)} async-done(((bf16[256,4,768]{0,2,1:T(8,128)(2,1)}), bf16[256,4,768]{0,2,1:T(8,128)(2,1)}, u32[]{:S(2)}, u32[]{:S(2)}) %all-to-all-start.4) | async-done | bytes 1572896 | tf_op jit(solution)/shard_map/all_to_all | solution.py:285
  210.8 2.6 copy.94
  213.4 5.7 fusion.77
  219.1 3.5 fusion.76
  222.6 6.7 %multiply_convert_fusion = (bf16[1024,768]{0,1:T(8,128)(2,1)S(1)}, bf16[1024,768]{0,1:T(8,128)(2,1)S(1)}, bf16[1024,768]{0,1:T(8,128)(2,1)}) fusion(f32[1024,768]{0,1:T(8,128)} %fusion.76, f32[1024,768]{0,1:T(8,128)} %fusion.77, bf16[1024,1024]{1,0:T(8,128)(2,1)} %all-gather.10.cloned.1.call-done, bf16[768,1024]{1,0:T(8,128)(2,1)S(1)} %copy-done), kind=kOutput, calls=%fused_computation.21 | convolution fusion | flops 1623195648 | bytes 14680064 | tf_op jit(solution)/shard_map/ro,io->ri/dot_general | solution.py:269
  231.8 3.2 add_convert_fusion.1
  235.1 31.5 %reduce-scatter.9.cloned.1.call-done = bf16[256,1024]{1,0:T(8,128)(2,1)} async-done(((bf16[1024,1024]{1,0:T(8,128)(2,1)}), bf16[256,1024]{1,0:T(8,128)(2,1)}) %reduce-scatter.9.cloned.1.call-update) | async-done | bytes 524304 | tf_op jit(solution)/shard_map/reduce_scatter | solution.py:281
  268.3 2.6 fusion.67
  271.0 22.7 %all-gather.12.cloned.1.call-done = bf16[1024,1024]{1,0:T(8,128)(2,1)} async-done(((bf16[256,1024]{1,0:T(8,128)(2,1)}), bf16[1024,1024]{1,0:T(8,128)(2,1)}) %all-gather.12.cloned.1.call-update) | async-done | bytes 2097168 | tf_op jit(solution)/shard_map/all_gather | solution.py:277
  293.7 3.1 convolution_convert_fusion.5
  296.9 8.5 %fusion.30 = bf16[2,128,1024]{2,1,0:T(8,128)(2,1)S(1)} fusion(bf16[1024,2,2,128]{0,3,2,1:T(8,128)(2,1)S(1)} %bitcast.254, f32[2,1024,1024,2]{2,1,3,0:T(8,128)} %copy-done.1, f32[2,2,1024]{2,1,0:T(2,128)S(1)} %log_add_fusion, pred[1024,1024]{0,1:T(8,128)(4,1)S(1)} %broadcast_compare_fusion), kind=kOutput, calls=%fused_computation.73 | convolution fusion | flops 1090781184 | bytes 19415040 | tf_op jit(solution)/shard_map/kgrt,rkgd->tkd/dot_general | solution.py:389
  305.5 12.5 %fusion = (f32[2,2,1024]{2,1,0:T(2,128)S(1)}, f32[2,1024,1024,2]{2,1,3,0:T(8,128)}) fusion(f32[2,1024,1024,2]{2,1,3,0:T(8,128)} %copy-done.1, f32[2,2,1024]{2,1,0:T(2,128)S(1)} %log_add_fusion, pred[1024,1024]{0,1:T(8,128)(4,1)S(1)} %broadcast_compare_fusion, bf16[1024,2,128,1]{0,2,3,1:T(8,128)(2,1)S(1)} %bitcast.257, bf16[1024,2,2,128]{0,3,2,1:T(8,128)(2,1)S(1)} %bitcast.255), kind=kOutput, calls=%fused_computation.2 | convolution fusion | flops 1094709248 | bytes 36208640 | tf_op jit(solution)/shard_map/rkgd,tkd->kgrt/dot_general | solution.py:388
  318.7 12.6 %fusion.2 = bf16[2,2,1024,1024]{2,3,1,0:T(8,128)(2,1)S(1)} fusion(f32[2,1024,1024,2]{2,1,3,0:T(8,128)} %get-tuple-element.89, f32[2,1024,1024,2]{2,1,3,0:T(8,128)} %copy-done.1, f32[2,2,1024]{2,1,0:T(2,128)S(1)} %get-tuple-element.88, f32[2,2,1024]{2,1,0:T(2,128)S(1)} %log_add_fusion, pred[1024,1024]{0,1:T(8,128)(4,1)S(1)} %broadcast_compare_fusion), kind=kLoop, calls=%fused_computation.4 | loop fusion | flops 25165824 | bytes 43024384 | tf_op jit(solution)/shard_map/convert_element_type | solution.py:393
  332.7 2.9 broadcast_multiply_fusion
  343.5 4.0 add_convert_fusion
  347.6 4.6 convolution_convert_fusion.2
  352.2 5.4 convolution_convert_fusion.3
  357.6 6.0 convolution_convert_fusion
  363.6 2.2 convolution_convert_fusion.4
  365.9 3.7 fusion.27
  369.6 213.4 %grad_sum.1 = (bf16[4,192,1024]{2,1,0:T(8,128)(2,1)}, bf16[256,6144]{1,0:T(8,128)(2,1)}, bf16[4,128,1024]{2,1,0:T(8,128)(2,1)}, bf16[256,4096]{1,0:T(8,128)(2,1)}) custom-call(bf16[4,192,1024]{2,1,0:T(8,128)(2,1)} %bitcast.249, bf16[4,256,1536]{2,1,0:T(8,128)(2,1)} %bitcast.237, bf16[4,128,1024]{2,1,0:T(8,128)(2,1)} %bitcast.250, bf16[4,256,1024]{2,1,0:T(8,128)(2,1)} %bitcast.244), custom_call_target="tpu_custom_call" | custom-call | tf_op jit(solution)/shard_map/grad_sum/pallas_call | solution.py:237
  583.0 4.7 reshape.491
  594.2 7.4 %reshape.494 = bf16[256,4,1536]{2,1,0:T(4,128)(2,1)} reshape(bf16[256,6144]{1,0:T(8,128)(2,1)} %get-tuple-element.31) | data formatting | bytes 6291456 | tf_op jit(solution)/shard_map/reshape | solution.py:427
  601.6 2.7 slice_convert_fusion
  614.2 39.5 %psum.7 = f32[2304]{0:T(1024)S(1)} all-reduce(f32[2304]{0:T(1024)S(1)} %pad_maximum_fusion.1), channel_id=1, replica_groups=mesh['shard'=4,'replica'=8] {'shard','replica'}, use_global_device_ids=true, to_apply=%region_19.20 | all-reduce | flops 2304 | bytes 18432 | tf_op jit(solution)/shard_map/psum | solution.py:437
  655.0 3.4 fusion.42
  (207 shorter events, 64.0 us)
Async XLA Ops:
  7.2 215.4 %copy-start = (bf16[768,1024]{1,0:T(8,128)(2,1)S(1)}, bf16[768,1024]{1,0:T(8,128)(2,1)}, u32[]{:S(2)}) copy-start(bf16[768,1024]{1,0:T(8,128)(2,1)} %param.31) | copy-start | bytes 4718596
  7.2 15.1 %copy-start.36 = (bf16[256,1024]{1,0:T(8,128)(2,1)S(1)}, bf16[256,1024]{1,0:T(8,128)(2,1)}, u32[]{:S(2)}) copy-start(bf16[256,1024]{1,0:T(8,128)(2,1)} %param.23) | copy-start | bytes 1572868
  7.2 66.6 %all-gather.6.cloned.1.call-start = ((), (), s32[]{:S(2)}) async-start(), calls=%async_computation.9 | async-start | bytes 2621440 | tf_op jit(solution)/shard_map/all_gather | solution.py:277
  8.6 2.7 copy-start.43
  8.7 14.8 %copy-start.41 = (f32[256]{0:T(256)}, f32[256]{0:T(256)S(1)}, u32[]{:S(2)}) copy-start(f32[256]{0:T(256)S(1)} %fusion.61) | copy-start | bytes 3076
  22.2 4.8 copy-start.37
  22.3 5.7 copy-start.40
  23.5 15.9 %all-to-all-start.1 = ((bf16[256,4,256]{2,0,1:T(8,128)(2,1)}), bf16[256,4,256]{2,0,1:T(8,128)(2,1)S(1)}, u32[]{:S(2)}, u32[]{:S(2)}) async-start(bf16[256,4,256]{2,0,1:T(8,128)(2,1)} %copy.83), calls=%async_computation.1 | async-start | bytes 1048576 | tf_op jit(solution)/shard_map/all_to_all | solution.py:285
  39.4 7.2 %copy-start.14 = (bf16[256,4,256]{2,0,1:T(8,128)(2,1)}, bf16[256,4,256]{2,0,1:T(8,128)(2,1)S(1)}, u32[]{:S(2)}) copy-start(bf16[256,4,256]{2,0,1:T(8,128)(2,1)S(1)} %all-to-all-done.1) | copy-start | bytes 1572868
  39.4 13.4 %all-to-all-start = ((bf16[256,4,256]{0,2,1:T(8,128)(2,1)}), bf16[256,4,256]{0,2,1:T(8,128)(2,1)}, u32[]{:S(2)}, u32[]{:S(2)}) async-start(bf16[256,4,256]{0,2,1:T(8,128)(2,1)} %bitcast.17), calls=%async_computation | async-start | bytes 1048576 | tf_op jit(solution)/shard_map/all_to_all | solution.py:285
  52.7 18.8 %all-to-all-start.2 = ((bf16[256,4,512]{2,0,1:T(8,128)(2,1)}), bf16[256,4,512]{2,0,1:T(8,128)(2,1)}, u32[]{:S(2)}, u32[]{:S(2)}) async-start(bf16[256,4,512]{2,0,1:T(8,128)(2,1)} %copy.86), calls=%async_computation.2 | async-start | bytes 2097152 | tf_op jit(solution)/shard_map/all_to_all | solution.py:285
  57.0 76.9 %reduce-scatter.5.cloned.1.call-start = ((), (), s32[]{:S(2)}) async-start(), calls=%async_computation.10 | async-start | bytes 2621440 | tf_op jit(solution)/shard_map/reduce_scatter | solution.py:281
  60.5 21.6 %copy-start.9 = (f32[1024,128]{0,1:T(8,128)}, f32[1024,128]{0,1:T(8,128)S(1)}, u32[]{:S(2)}) copy-start(f32[1024,128]{0,1:T(8,128)S(1)} %get-tuple-element.65) | copy-start | bytes 1572868
  76.2 4.3 copy-start.5
  76.3 2.3 copy-start.45
  82.9 3.4 copy-start.17
  86.3 5.8 copy-start.1
  86.3 3.7 copy-start.19
  90.8 7.3 %copy-start.32 = (bf16[1024,256]{0,1:T(8,128)(2,1)}, bf16[1024,256]{0,1:T(8,128)(2,1)S(1)}, u32[]{:S(2)}) copy-start(bf16[1024,256]{0,1:T(8,128)(2,1)S(1)} %convolution_convert_fusion.7) | copy-start | bytes 1572868
  92.0 6.1 copy-start.50
  102.0 31.9 %copy-start.4 = (bf16[1,256,1024]{2,1,0:T(8,128)(2,1)S(1)}, bf16[1,256,1024]{2,1,0:T(8,128)(2,1)}, u32[]{:S(2)}) copy-start(bf16[1,256,1024]{2,1,0:T(8,128)(2,1)} %param.17) | copy-start | bytes 1572868
  102.0 111.4 %all-gather.8.cloned.1.call-start = ((), (), s32[]{:S(2)}) async-start(), calls=%async_computation.11 | async-start | bytes 2621440 | tf_op jit(solution)/shard_map/all_gather | solution.py:277
  139.8 35.6 %all-to-all-start.3 = ((bf16[256,4,768]{0,2,1:T(8,128)(2,1)}), bf16[256,4,768]{0,2,1:T(8,128)(2,1)}, u32[]{:S(2)}, u32[]{:S(2)}) async-start(bf16[256,4,768]{0,2,1:T(8,128)(2,1)} %bitcast.224), calls=%async_computation.4 | async-start | bytes 3145728 | tf_op jit(solution)/shard_map/all_to_all | solution.py:285
  144.2 78.4 %all-gather.10.cloned.1.call-start = ((), (), s32[]{:S(2)}) async-start(), calls=%async_computation.13 | async-start | bytes 2621440 | tf_op jit(solution)/shard_map/all_gather | solution.py:277
  175.4 35.4 %all-to-all-start.4 = ((bf16[256,4,768]{0,2,1:T(8,128)(2,1)}), bf16[256,4,768]{0,2,1:T(8,128)(2,1)}, u32[]{:S(2)}, u32[]{:S(2)}) async-start(bf16[256,4,768]{0,2,1:T(8,128)(2,1)} %bitcast.225), calls=%async_computation.5 | async-start | bytes 3145728 | tf_op jit(solution)/shard_map/all_to_all | solution.py:285
  179.8 86.9 %reduce-scatter.9.cloned.1.call-start = ((), (), s32[]{:S(2)}) async-start(), calls=%async_computation.14 | async-start | bytes 2621440 | tf_op jit(solution)/shard_map/reduce_scatter | solution.py:281
  213.4 5.7 copy-start.26
  213.4 5.7 copy-start.47
  222.6 6.7 %copy-start.27 = (bf16[4,256,768]{2,1,0:T(8,128)(2,1)S(1)}, bf16[4,256,768]{2,1,0:T(8,128)(2,1)}, u32[]{:S(2)}) copy-start(bf16[4,256,768]{2,1,0:T(8,128)(2,1)} %copy.92) | copy-start | bytes 4718596
  229.3 2.5 copy-start.28
  235.0 58.7 %all-gather.12.cloned.1.call-start = ((), (), s32[]{:S(2)}) async-start(), calls=%async_computation.15 | async-start | bytes 2621440 | tf_op jit(solution)/shard_map/all_gather | solution.py:277
  271.0 341.7 %reduce-scatter.11.cloned.1.call-start = ((), (), s32[]{:S(2)}) async-start(), calls=%async_computation.16 | async-start | bytes 2621440 | tf_op jit(solution)/shard_map/reduce_scatter | solution.py:281
  296.9 8.6 %copy-start.33 = (bf16[1024,256]{0,1:T(8,128)(2,1)S(1)}, bf16[1024,256]{0,1:T(8,128)(2,1)}, u32[]{:S(2)}) copy-start(bf16[1024,256]{0,1:T(8,128)(2,1)} %copy-done.32) | copy-start | bytes 1572868
  305.4 12.5 %copy-start.34 = (bf16[2,128,1024]{2,1,0:T(8,128)(2,1)}, bf16[2,128,1024]{2,1,0:T(8,128)(2,1)S(1)}, u32[]{:S(2)}) copy-start(bf16[2,128,1024]{2,1,0:T(8,128)(2,1)S(1)} %fusion.30) | copy-start | bytes 1572868
  305.4 12.5 %copy-start.20 = (bf16[4,256,256]{2,1,0:T(8,128)(2,1)S(1)}, bf16[4,256,256]{2,1,0:T(8,128)(2,1)}, u32[]{:S(2)}) copy-start(bf16[4,256,256]{2,1,0:T(8,128)(2,1)} %copy.81) | copy-start | bytes 1572868
  318.7 12.6 %copy-start.25 = (bf16[1024,2,128,1]{0,2,3,1:T(8,128)(2,1)S(1)}, bf16[1024,2,128,1]{0,2,3,1:T(8,128)(2,1)}, u32[]{:S(2)}) copy-start(bf16[1024,2,128,1]{0,2,3,1:T(8,128)(2,1)} %copy-done.24) | copy-start | bytes 1572868
  347.6 307.4 %reduce-scatter.7.cloned.1.call-start = ((), (), s32[]{:S(2)}) async-start(), calls=%async_computation.12 | async-start | bytes 2621440 | tf_op jit(solution)/shard_map/reduce_scatter | solution.py:281
  352.2 5.4 copy-start.48
  352.2 5.4 copy-start.53
  352.2 5.4 copy-start.55
  357.6 6.0 copy-start.49
  357.6 6.0 copy-start.51
  363.6 2.3 copy-start.22
  363.6 2.3 copy-start.35
  363.6 2.3 copy-start.46
  610.5 44.4 %copy-start.44 = (f32[256]{0:T(256)S(1)}, f32[256]{0:T(256)}, u32[]{:S(2)}) copy-start(f32[256]{0:T(256)} %copy-done.43) | copy-start | bytes 3076
  610.5 44.5 %copy-start.7 = (bf16[256,1024]{1,0:T(8,128)(2,1)S(1)}, bf16[256,1024]{1,0:T(8,128)(2,1)}, u32[]{:S(2)}) copy-start(bf16[256,1024]{1,0:T(8,128)(2,1)} %reduce-scatter.5.cloned.1.call-done) | copy-start | bytes 1572868
  610.5 44.5 %copy-start.13 = (bf16[1,256,1024]{2,1,0:T(8,128)(2,1)S(1)}, bf16[1,256,1024]{2,1,0:T(8,128)(2,1)}, u32[]{:S(2)}) copy-start(bf16[1,256,1024]{2,1,0:T(8,128)(2,1)} %param.18) | copy-start | bytes 1572868
  (21 other events, 34.4 us)
Sparse Core Ops, SparseCore 0:
  22.4 26.2 all-gather.5
  102.1 31.7 reduce-scatter.4
  137.4 33.8 all-gather.7
  172.7 33.7 all-gather.9
  235.2 31.4 reduce-scatter.8
  271.1 22.5 all-gather.11
  347.7 31.4 reduce-scatter.10
  381.8 31.3 reduce-scatter.6

commit v3 on v2

--- a/solution.py
+++ b/solution.py
@@ -1,5 +1,8 @@
+import functools
+
 import jax
 import jax.numpy as jnp
+import numpy as np
 from jax import lax
 from jax.experimental import pallas as pl
 from jax.experimental.pallas import tpu as pltpu
@@ -9,6 +12,7 @@
 ROPE_BASE = 1000000.0
 BF = jnp.bfloat16
 F32 = jnp.float32
+MESH = pl.DeviceIdType.MESH
 
 
 class Topo:
@@ -240,53 +244,591 @@
     return call
 
 
-def rms_scale(values, gain_vec):
-    return (
-        values * lax.rsqrt(jnp.mean(values * values, axis=-1, keepdims=True) + EPSILON) * gain_vec
-    )
-
-
-def rotate_half(values, cosine, sine_table):
-    middle = values.shape[-1] // 2
-    turned = jnp.concatenate([-values[..., middle:], values[..., :middle]], axis=-1)
-    return values * cosine + turned * sine_table
-
-
-def rotary_tables(position, head_width):
+class Net:
+    def __init__(self, tp, send, recv):
+        self.tp = tp
+        self.send = send
+        self.recv = recv
+        self.k = 0
+        self.live = []
+
+    def slot(self):
+        self.k += 1
+        return self.k - 1
+
+    def make(self, slot, src, dst, dev):
+        return pltpu.make_async_remote_copy(
+            src, dst, self.send.at[slot], self.recv.at[slot], device_id=dev, device_id_type=MESH
+        )
+
+    def push(self, slot, src, dst, dev):
+        c = self.make(slot, src, dst, dev)
+        c.start()
+        self.live.append(c)
+        return c
+
+    def arrived(self, slot, ref):
+        self.make(slot, ref, ref, self.tp.sh(1)).wait_recv()
+
+    def drain(self):
+        for c in self.live:
+            c.wait_send()
+        self.live = []
+
+
+def dot(a, b, ca=1, cb=0):
+    return lax.dot_general(a, b, (((ca,), (cb,)), ((), ())), preferred_element_type=F32)
+
+
+def rows_of(t, rows, ch=0, ch_rows=None):
+    n = rows if ch_rows is None else ch_rows
+    start = t * rows + ch * n
+    return pl.ds(start if isinstance(start, int) else pl.multiple_of(start, 128), n)
+
+
+def fold8(v):
+    out = v[0:8]
+    for k in range(1, v.shape[0] // 8):
+        out = out + v[8 * k : 8 * k + 8]
+    return out
+
+
+def layer_sizes(tokens, query_weight, key_weight, gate_weight, query_gain, shards):
+    z = {}
+    z["own"] = tokens.shape[0]
+    z["D"] = tokens.shape[1]
+    z["T"] = z["own"] * shards
+    z["HD"] = query_gain.shape[0] * shards
+    z["QW"] = query_weight.shape[1] // shards
+    z["KW"] = key_weight.shape[1] // shards
+    z["FW"] = gate_weight.shape[1] // shards
+    return z
+
+
+def layer_call(z, S, R, args):
+    own, D, T, HD, QW, KW, FW = (z[k] for k in ("own", "D", "T", "HD", "QW", "KW", "FW"))
+    QKV = QW + 2 * KW
+    QK = QW + KW
+    heads, kvs = QW // HD, KW // HD
+    per = heads // kvs
+    BLK = 128
+    CH = 128
+    NCH = own // CH
+    TILE = 256
+    scale = float(HD) ** -0.5
+    SUB = 32
+    GW = 2 * D + 2 * HD
+
+    vm = lambda shape, dtype: pltpu.VMEM(shape, dtype)
+    scratch = [
+        vm((T // BLK, BLK, D), BF), vm((T // BLK, BLK, D), BF), vm((T // BLK, BLK, D), BF), vm((T // BLK, BLK, D), BF), vm((T, D), BF),
+        vm((D, QKV), BF), vm((D, 2 * FW), BF), vm((QW, D), BF), vm((FW, D), BF),
+        vm((S, 8, GW), F32), vm((8, GW), F32), vm((T, 2 * HD), F32),
+        vm((T, QK), F32), vm((T, QKV), BF), vm((T, HD), F32), vm((T // BLK, BLK, QW), BF), vm((T, QW), BF),
+        vm((2, NCH, CH, D), BF), vm((2, NCH, CH, D), BF), vm((NCH, CH, D), BF), vm((2, NCH, CH, D), BF),
+        vm((NCH, CH, D), F32), vm((NCH, CH, D), F32), vm((own, D), F32), vm((own, D), BF),
+        vm((T, FW), BF), vm((T, 2 * FW), BF), vm((T // BLK, BLK, QKV), BF), vm((T, QW), BF), vm((T, 2 * KW), F32),
+        vm((own, FW), F32), vm((T, HD), F32), vm((8, GW), F32), vm((own, 2 * FW), F32),
+        vm((own, D), BF), vm((own, D), F32),
+        vm((FW, D), BF), vm((D, 2 * FW), BF), vm((QW, D), BF), vm((D, QKV), BF),
+        pltpu.SemaphoreType.DMA((140,)), pltpu.SemaphoreType.DMA((140,)), pltpu.SemaphoreType.DMA((24,)),
+    ]
+    outs = [
+        ((own, D), BF), ((own, D), F32), ((8, GW), F32),
+        ((FW, D), BF), ((D, 2 * FW), BF), ((QW, D), BF), ((D, QKV), BF),
+    ]
+
+    def body(*refs):
+        meta, tok_in, cot_in, gains_in, cs_in, wq_in, wk_in, wv_in, wo_in, wg_in, wu_in, wd_in = refs[:12]
+        out_o, dx_o, gg_o, gd_o, ggu_o, go_o, gqkv_o = refs[12:19]
+        (TOK, GB, N2, GMI, NP, WQKV, WGU, WO, WD, GAIN, GV, CS, RAW, HEADS, LSE, MIXP, MIXS,
+         SBC, RBC, SBY, RBYS, HY, HO, HID, GH, ACT, DGU, DQKV, GMP, DKV, DQ, DQH, GG, X, OUTB, DX,
+         GD, GGU, GO, GQKV, send, recv, lsem) = refs[19:]
+        round_no = [0]
+        tp = Topo(S, R)
+        net = Net(tp, send, recv)
+        s = tp.s
+        lk = [0]
+        locals_live = []
+
+        def local(src, dst):
+            c = pltpu.make_async_copy(src, dst, lsem.at[lk[0]])
+            lk[0] += 1
+            c.start()
+            return c
+
+        me = rows_of(s, own)
+        c_tok = [local(tok_in.at[ch * CH : (ch + 1) * CH], TOK.at[NCH * s + ch]) for ch in range(NCH)]
+        c_cot = local(cot_in, GH)
+        c_gain = local(gains_in, GAIN.at[0])
+        c_cs = local(cs_in, CS)
+        c_wo = local(wo_in, WO)
+        c_wd = local(wd_in, WD)
+
+        def wcols(t):
+            return (
+                (wq_in, t * QW, QW, WQKV, 0),
+                (wk_in, t * KW, KW, WQKV, QW),
+                (wv_in, t * KW, KW, WQKV, QK),
+                (wg_in, t * FW, FW, WGU, 0),
+                (wu_in, t * FW, FW, WGU, FW),
+            )
+
+        c_w = []
+        for ref, at, w, dst, to in wcols(s):
+            c_w.append(
+                local(ref.at[:, pl.ds(pl.multiple_of(at, 128), w)], dst.at[me, to : to + w])
+            )
+        barrier(tp)
+        g_slot = [net.slot() for _ in range(3)]
+        for k in (1, 2, 3):
+            net.push(g_slot[k - 1], gains_in, GAIN.at[k], tp.sh(k))
+        gath = {}
+
+        def ag_push(name, buf, ch, src=None):
+            r = NCH * s + ch
+            k1, k2, k3 = net.slot(), net.slot(), net.slot()
+            gath[name, ch] = (k1, k2, k3)
+            src = buf.at[r] if src is None else src
+            net.push(k2, src, buf.at[r], tp.sh(2))
+            net.push(k1, src, buf.at[r], tp.sh(1))
+
+        def ag_relay(name, buf, ch):
+            k1, k2, k3 = gath[name, ch]
+            r = NCH * (s ^ 2) + ch
+            net.arrived(k2, buf.at[r])
+            net.push(k3, buf.at[r], buf.at[r], tp.sh(1))
+
+        def ag_near(name, buf, ch):
+            net.arrived(gath[name, ch][0], buf.at[NCH * (s ^ 1) + ch])
+
+        def ag_far(name, buf, ch):
+            net.arrived(gath[name, ch][2], buf.at[NCH * (s ^ 3) + ch])
+
+        for ch in range(NCH):
+            ag_push("tok", TOK, ch, tok_in.at[ch * CH : (ch + 1) * CH])
+        half = own // 2
+        hb = tp.b * half
+        wsl = {}
+
+        def w_push(lo, hi):
+            for k in (2, 3, 1):
+                t = s ^ k
+                for j, (ref, at, w, dst, to) in enumerate(wcols(t)):
+                    if not lo <= j < hi:
+                        continue
+                    wsl[k, j] = net.slot()
+                    cols = pl.ds(pl.multiple_of(at, 128), w)
+                    if k == 1:
+                        net.push(wsl[k, j], ref.at[:, cols], dst.at[me, to : to + w], tp.sh(k))
+                    else:
+                        src = ref.at[pl.ds(pl.multiple_of(hb, 128), half), cols]
+                        r = pl.ds(pl.multiple_of(s * own + hb, 128), half)
+                        net.push(wsl[k, j], src, dst.at[r, to : to + w], tp.sh(k))
+
+        def w_relay(lo, hi):
+            for k in (2, 3):
+                for j, (ref, at, w, dst, to) in enumerate(wcols(s)):
+                    if not lo <= j < hi:
+                        continue
+                    r = pl.ds(pl.multiple_of((s ^ k) * own + hb, 128), half)
+                    part = dst.at[r, to : to + w]
+                    net.arrived(wsl[k, j], part)
+                    wsl[k + 2, j] = net.slot()
+                    net.push(wsl[k + 2, j], part, part, tp.rep(tp.r ^ 1))
+
+        def w_wait(lo, hi):
+            for j, (ref, at, w, dst, to) in enumerate(wcols(s)):
+                if not lo <= j < hi:
+                    continue
+                net.arrived(wsl[1, j], dst.at[rows_of(s ^ 1, own), to : to + w])
+                for k in (2, 3):
+                    r = pl.ds(pl.multiple_of((s ^ k) * own + (half - hb), 128), half)
+                    net.arrived(wsl[k + 2, j], dst.at[r, to : to + w])
+
+        w_push(0, 3)
+        w_push(3, 5)
+        c_cot.wait()
+        length = meta[16]
+        for ch in range(NCH):
+            blk = meta[NCH * s + ch]
+            def cot_rows(u, _, ch=ch, blk=blk):
+                q = pl.multiple_of(u * SUB, SUB)
+                pos = blk * BLK + q + lax.broadcasted_iota(jnp.int32, (SUB, D), 0)
+                g = GH[pl.ds(ch * CH + q, SUB), :].astype(F32)
+                GB[NCH * s + ch, pl.ds(q, SUB), :] = jnp.where(pos < length, g, 0.0).astype(BF)
+                return 0
+
+            lax.fori_loop(0, CH // SUB, cot_rows, 0)
+            ag_push("gb", GB, ch)
+        c_gain.wait()
+        for k in (1, 2, 3):
+            net.arrived(g_slot[k - 1], GAIN.at[k])
+        GV[...] = GAIN[0] + GAIN[1] + GAIN[2] + GAIN[3]
+        gain1 = GV[0:1, 0:D]
+        gain2 = GV[0:1, D : 2 * D]
+        gq = GV[0:1, 2 * D : 2 * D + HD]
+        gk = GV[0:1, 2 * D + HD : GW]
+        GG[...] = jnp.zeros_like(GG)
+        DKV[...] = jnp.zeros_like(DKV)
+
+        for c in c_tok:
+            c.wait()
+        for c in c_w:
+            c.wait()
+        for ch in range(NCH):
+            ag_relay("tok", TOK, ch)
+        w_relay(0, 3)
+        for ch in range(NCH):
+            ag_near("tok", TOK, ch)
+            ag_far("tok", TOK, ch)
+
+        def norm1(i, _):
+            src = meta[8 + i]
+
+            def sub(u, _):
+                x = TOK[src, pl.ds(pl.multiple_of(u * SUB, SUB), SUB), :].astype(F32)
+                r = lax.rsqrt(jnp.mean(x * x, axis=1, keepdims=True) + EPSILON)
+                NP[pl.ds(pl.multiple_of(i * BLK + u * SUB, SUB), SUB), :] = (x * r * gain1).astype(BF)
+                return 0
+
+            return lax.fori_loop(0, BLK // SUB, sub, 0)
+
+        lax.fori_loop(0, T // BLK, norm1, 0)
+        w_wait(0, 3)
+        c_cs.wait()
+
+        def proj(i, _):
+            r = rows_of(i, TILE)
+            raw = dot(NP[r, :], WQKV[...])
+            RAW[r, :] = raw[:, :QK]
+            HEADS[r, QK:] = raw[:, QK:].astype(BF)
+
+            def sub(u, _):
+                rr = pl.ds(pl.multiple_of(i * TILE + u * SUB, SUB), SUB)
+                co = CS[rr, 0:HD]
+                si = CS[rr, HD : 2 * HD]
+                for h in range(heads + kvs):
+                    g = gq if h < heads else gk
+                    v = RAW[rr, h * HD : (h + 1) * HD]
+                    n = v * lax.rsqrt(jnp.mean(v * v, axis=1, keepdims=True) + EPSILON) * g
+                    HEADS[rr, h * HD : (h + 1) * HD] = (
+                        n * co + pltpu.roll(n, HD // 2, 1) * si
+                    ).astype(BF)
+                return 0
+
+            return lax.fori_loop(0, TILE // SUB, sub, 0)
+
+        lax.fori_loop(0, T // TILE, proj, 0)
+
+        lane = lax.broadcasted_iota(jnp.int32, (TILE, HD), 1)
+        tri = lax.broadcasted_iota(jnp.int32, (TILE, TILE), 1) <= lax.broadcasted_iota(
+            jnp.int32, (TILE, TILE), 0
+        )
+
+        def masked_scores(q, h_kv_cols, i):
+            k = HEADS[0 : (i + 1) * TILE, h_kv_cols]
+            sc = dot(q, k, 1, 1) * scale
+            last = jnp.where(tri, sc[:, i * TILE :], -1e30)
+            return last if i == 0 else jnp.concatenate([sc[:, : i * TILE], last], axis=1)
+
+        def head_cols(h):
+            return pl.ds(pl.multiple_of(h * HD, HD), HD)
+
+        def attend(h, _):
+            kv = h // per if isinstance(h, int) else lax.div(h, per)
+            kc = pl.ds(pl.multiple_of(QW + kv * HD, HD), HD)
+            vc = pl.ds(pl.multiple_of(QK + kv * HD, HD), HD)
+            for i in range(T // TILE):
+                r = rows_of(i, TILE)
+                sc = masked_scores(HEADS[r, head_cols(h)], kc, i)
+                top = jnp.max(sc, axis=1, keepdims=True)
+                e = jnp.exp(sc - top)
+                total = jnp.sum(e, axis=1, keepdims=True)
+                o = dot(e.astype(BF), HEADS[0 : (i + 1) * TILE, vc]) / total
+                MIXP[i * (TILE // BLK) : (i + 1) * (TILE // BLK), :, head_cols(h)] = o.astype(BF).reshape(
+                    TILE // BLK, BLK, HD
+                )
+                lse = top + jnp.log(total)
+                LSE[r, :] = jnp.where(lane == h, lse, LSE[r, :])
+            return 0
+
+        LSE[...] = jnp.zeros_like(LSE)
+        lax.fori_loop(0, heads, attend, 0)
+        c_wo.wait()
+
+        def reduce_scatter(partial):
+            c_slot = [[net.slot() for _ in range(NCH)] for _ in range(2)]
+            y_slot = [net.slot() for _ in range(NCH)]
+            round_no[0] += 1
+            RBY = RBYS.at[round_no[0] % 2]
+            for ch in range(NCH):
+                SBC[0, ch] = partial(s ^ 3, ch).astype(BF)
+                net.push(c_slot[0][ch], SBC.at[0, ch], RBC.at[0, ch], tp.sh(1))
+            for ch in range(NCH):
+                HY[ch] = partial(s ^ 2, ch)
+            for ch in range(NCH):
+                net.arrived(c_slot[0][ch], RBC.at[0, ch])
+                SBY[ch] = (HY[ch] + RBC[0, ch].astype(F32)).astype(BF)
+                net.push(y_slot[ch], SBY.at[ch], RBY.at[ch], tp.sh(2))
+            for ch in range(NCH):
+                SBC[1, ch] = partial(s ^ 1, ch).astype(BF)
+                net.push(c_slot[1][ch], SBC.at[1, ch], RBC.at[1, ch], tp.sh(1))
+            for ch in range(NCH):
+                HO[ch] = partial(s, ch)
+            for ch in range(NCH):
+                net.arrived(c_slot[1][ch], RBC.at[1, ch])
+                HO[ch] = HO[ch] + RBC[1, ch].astype(F32)
+            return y_slot
+
+        def rs_finish(y_slot, ch):
+            RBY = RBYS.at[round_no[0] % 2]
+            net.arrived(y_slot[ch], RBY.at[ch])
+            HO[ch] = HO[ch] + RBY[ch].astype(F32)
+
+        def mixed_rows(t, ch):
+            src = meta[NCH * t + ch]
+            v = MIXP[src]
+            MIXS[rows_of(t, own, ch, CH), :] = v
+            return dot(v, WO[...])
+
+        w_relay(3, 5)
+        ys = reduce_scatter(mixed_rows)
+        for ch in range(NCH):
+            ag_relay("gb", GB, ch)
+        for ch in range(NCH):
+            rs_finish(ys, ch)
+
+            def norm2(u, _, ch=ch):
+                q = pl.ds(pl.multiple_of(u * SUB, SUB), SUB)
+                x = TOK[NCH * s + ch, q, :].astype(F32) + HO[ch, q, :]
+                HID[pl.ds(pl.multiple_of(ch * CH + u * SUB, SUB), SUB), :] = x
+                r = lax.rsqrt(jnp.mean(x * x, axis=1, keepdims=True) + EPSILON)
+                N2[NCH * s + ch, q, :] = (x * r * gain2).astype(BF)
+                return 0
+
+            lax.fori_loop(0, CH // SUB, norm2, 0)
+            ag_push("n2", N2, ch)
+        c_wd.wait()
+        w_wait(3, 5)
+        for ch in range(NCH):
+            ag_near("gb", GB, ch)
+            ag_far("gb", GB, ch)
+
+        def ffn(t):
+            two = pl.ds(NCH * t, NCH)
+            X[...] = dot(N2[two].reshape(own, D), WGU[...])
+            DQ[...] = dot(GB[two].reshape(own, D), WD[...], 1, 1)
+
+            def sub(u, _):
+                q = pl.ds(pl.multiple_of(u * SUB, SUB), SUB)
+                at = pl.ds(pl.multiple_of(t * own + u * SUB, SUB), SUB)
+                for c in range(0, FW, 256):
+                    gate = X[q, c : c + 256]
+                    up = X[q, FW + c : FW + c + 256]
+                    ga = DQ[q, c : c + 256]
+                    sig = 1.0 / (1.0 + jnp.exp(-gate))
+                    act = gate * sig
+                    ACT[at, c : c + 256] = (act * up).astype(BF)
+                    DGU[at, c : c + 256] = (ga * up * (sig * (1.0 + gate * (1.0 - sig)))).astype(BF)
+                    DGU[at, FW + c : FW + c + 256] = (ga * act).astype(BF)
+                return 0
+
+            lax.fori_loop(0, own // SUB, sub, 0)
+
+        ffn(s)
+        for ch in range(NCH):
+            ag_near("n2", N2, ch)
+        ffn(s ^ 1)
+        for ch in range(NCH):
+            ag_relay("n2", N2, ch)
+        ffn(s ^ 2)
+        for ch in range(NCH):
+            ag_far("n2", N2, ch)
+        ffn(s ^ 3)
+        net.drain()
+
+        ys = reduce_scatter(
+            lambda t, ch: dot(DGU[rows_of(t, own, ch, CH), :], WGU[...], 1, 1)
+        )
+
+        def wgrad(left, right, out, lw, rw):
+            def step(i, _):
+                cols = pl.ds(pl.multiple_of(i * 256, 256), 256)
+                lhs = left[:, :, cols] if len(left.shape) == 3 else left[:, cols]
+                rhs = right[...].reshape(T, rw)
+                out[cols, :] = dot(lhs.reshape(T, 256), rhs, 0, 0).astype(BF)
+                return 0
+
+            lax.fori_loop(0, lw // 256, step, 0)
+
+        wgrad(ACT, GB, GD, FW, D)
+        for ch in range(NCH):
+            rs_finish(ys, ch)
+
+            def norm2_back(u, acc, ch=ch):
+                q = pl.ds(pl.multiple_of(u * SUB, SUB), SUB)
+                qo = pl.ds(pl.multiple_of(ch * CH + u * SUB, SUB), SUB)
+                x = HID[qo, :]
+                du = HO[ch, q, :]
+                r = lax.rsqrt(jnp.mean(x * x, axis=1, keepdims=True) + EPSILON)
+                gd = du * gain2
+                m = jnp.mean(x * gd, axis=1, keepdims=True)
+                gh = GB[NCH * s + ch, q, :].astype(F32) + r * gd - x * (r * r * r * m)
+                DX[qo, :] = gh
+                GMI[NCH * s + ch, q, :] = gh.astype(BF)
+                GG[:, D : 2 * D] = GG[:, D : 2 * D] + fold8(du * x * r)
+                return acc
+
+            lax.fori_loop(0, CH // SUB, norm2_back, 0)
+            ag_push("gmi", GMI, ch)
+        wgrad(N2, DGU, GGU, D, 2 * FW)
+        for ch in range(NCH):
+            ag_relay("gmi", GMI, ch)
+        for ch in range(NCH):
+            ag_near("gmi", GMI, ch)
+            ag_far("gmi", GMI, ch)
+
+        def gmix(i, _):
+            a = GMI[meta[8 + 2 * i]]
+            b = GMI[meta[9 + 2 * i]]
+            GMP[rows_of(i, TILE), :] = dot(
+                jnp.concatenate([a, b], axis=0), WO[...], 1, 1
+            ).astype(BF)
+            return 0
+
+        lax.fori_loop(0, T // TILE, gmix, 0)
+        wgrad(MIXS, GMI, GO, QW, D)
+        net.drain()
+        ys = reduce_scatter(lambda t, ch: dot(ACT[rows_of(t, own, ch, CH), :], WD[...]))
+
+        def head_back(v, du, g):
+            r = lax.rsqrt(jnp.mean(v * v, axis=1, keepdims=True) + EPSILON)
+            gd = du * g
+            m = jnp.mean(v * gd, axis=1, keepdims=True)
+            return r * gd - v * (r * r * r * m), fold8(du * v * r)
+
+        def unrotate(g, rr):
+            return g * CS[rr, 0:HD] + pltpu.roll(g * CS[rr, HD : 2 * HD], HD // 2, 1)
+
+        def attend_back(h, _):
+            kv = lax.div(h, per)
+            kc = pl.ds(pl.multiple_of(QW + kv * HD, HD), HD)
+            vc = pl.ds(pl.multiple_of(QK + kv * HD, HD), HD)
+            dk = pl.ds(pl.multiple_of(kv * HD, HD), HD)
+            dv = pl.ds(pl.multiple_of(KW + kv * HD, HD), HD)
+            for i in range(T // TILE):
+                r = rows_of(i, TILE)
+                n = (i + 1) * TILE
+                q = HEADS[r, head_cols(h)]
+                gm = GMP[r, head_cols(h)]
+                lse = jnp.sum(jnp.where(lane == h, LSE[r, :], 0.0), axis=1, keepdims=True)
+                p = jnp.exp(masked_scores(q, kc, i) - lse)
+                gp = dot(gm, HEADS[0:n, vc], 1, 1)
+                inner = jnp.sum(p * gp, axis=1, keepdims=True)
+                ds = (p * (gp - inner)).astype(BF)
+                DKV[0:n, dv] = DKV[0:n, dv] + dot(p.astype(BF), gm, 0, 0)
+                DKV[0:n, dk] = DKV[0:n, dk] + dot(ds, q, 0, 0) * scale
+                DQH[r, :] = dot(ds, HEADS[0:n, kc]) * scale
+            def sub(u, _):
+                rr = pl.ds(pl.multiple_of(u * SUB, SUB), SUB)
+                lr = pl.ds(pl.multiple_of(lax.rem(u, BLK // SUB) * SUB, SUB), SUB)
+                d, gg = head_back(RAW[rr, head_cols(h)], unrotate(DQH[rr, :], rr), gq)
+                DQKV[lax.div(u, BLK // SUB), lr, head_cols(h)] = d.astype(BF)
+                GG[:, 2 * D : 2 * D + HD] = GG[:, 2 * D : 2 * D + HD] + gg
+                return 0
+
+            lax.fori_loop(0, T // SUB, sub, 0)
+            return 0
+
+        lax.fori_loop(0, heads, attend_back, 0)
+
+        def key_back(u, _):
+            rr = pl.ds(pl.multiple_of(u * SUB, SUB), SUB)
+            lb = lax.div(u, BLK // SUB)
+            lr = pl.ds(pl.multiple_of(lax.rem(u, BLK // SUB) * SUB, SUB), SUB)
+            for kv in range(kvs):
+                c = slice(QW + kv * HD, QW + (kv + 1) * HD)
+                d, gg = head_back(
+                    RAW[rr, c], unrotate(DKV[rr, kv * HD : (kv + 1) * HD], rr), gk
+                )
+                DQKV[lb, lr, c] = d.astype(BF)
+                GG[:, 2 * D + HD : GW] = GG[:, 2 * D + HD : GW] + gg
+            DQKV[lb, lr, QK:QKV] = DKV[rr, KW : 2 * KW].astype(BF)
+            return 0
+
+        lax.fori_loop(0, T // SUB, key_back, 0)
+        for ch in range(NCH):
+            rs_finish(ys, ch)
+
+            def out_rows(u, _, ch=ch):
+                q = pl.ds(pl.multiple_of(u * SUB, SUB), SUB)
+                qo = pl.ds(pl.multiple_of(ch * CH + u * SUB, SUB), SUB)
+                OUTB[qo, :] = (HID[qo, :] + HO[ch, q, :]).astype(BF)
+                return 0
+
+            lax.fori_loop(0, CH // SUB, out_rows, 0)
+        c_out = local(OUTB, out_o)
+        net.drain()
+
+        def back_rows(t, ch):
+            src = meta[NCH * t + ch]
+            return dot(DQKV[src], WQKV[...], 1, 1)
+
+        ys = reduce_scatter(back_rows)
+
+        def wgrad_qkv(i, _):
+            cols = pl.ds(pl.multiple_of(i * 256, 256), 256)
+            GQKV[cols, :] = dot(NP[:, cols], DQKV[...].reshape(T, QKV), 0, 0).astype(BF)
+            return 0
+
+        lax.fori_loop(0, D // 256, wgrad_qkv, 0)
+        for ch in range(NCH):
+            rs_finish(ys, ch)
+
+            def norm1_back(u, acc, ch=ch):
+                q = pl.ds(pl.multiple_of(u * SUB, SUB), SUB)
+                qo = pl.ds(pl.multiple_of(ch * CH + u * SUB, SUB), SUB)
+                x = TOK[NCH * s + ch, q, :].astype(F32)
+                du = HO[ch, q, :]
+                r = lax.rsqrt(jnp.mean(x * x, axis=1, keepdims=True) + EPSILON)
+                gd = du * gain1
+                m = jnp.mean(x * gd, axis=1, keepdims=True)
+                DX[qo, :] = DX[qo, :] + r * gd - x * (r * r * r * m)
+                GG[:, 0:D] = GG[:, 0:D] + fold8(du * x * r)
+                return acc
+
+            lax.fori_loop(0, CH // SUB, norm1_back, 0)
+        c_dx = local(DX, dx_o)
+        c_gg = local(GG, gg_o)
+        cg = [local(a, b) for a, b in ((GD, gd_o), (GGU, ggu_o), (GO, go_o), (GQKV, gqkv_o))]
+        for c in [c_out, c_dx, c_gg] + cg:
+            c.wait()
+        net.drain()
+
+    any_ = pl.BlockSpec(memory_space=pl.ANY)
+    specs = [pl.BlockSpec(memory_space=pltpu.SMEM)] + [any_] * 11
+    return pl.pallas_call(
+        body,
+        out_shape=[jax.ShapeDtypeStruct(*o) for o in outs],
+        in_specs=specs,
+        out_specs=[any_] * len(outs),
+        scratch_shapes=scratch,
+        compiler_params=pltpu.CompilerParams(
+            collective_id=2, has_side_effects=True, vmem_limit_bytes=64 << 20
+        ),
+        name="layer",
+    )(*args)
+
+
+def rotary_table(slot_len, head_width):
     middle = head_width // 2
-    exponent = jnp.arange(middle, dtype=F32) * 2.0 / head_width
-    inverse = ROPE_BASE ** (-exponent)
-    phases = position.astype(F32)[..., None] * inverse
-    phases = jnp.concatenate([phases, phases], axis=-1)
-    return (jnp.cos(phases), jnp.sin(phases))
-
-
-def mm(a, b):
-    return jnp.einsum("ri,io->ro", a, b, preferred_element_type=F32)
-
-
-def mm_t(a, b):
-    return jnp.einsum("ro,io->ri", a, b, preferred_element_type=F32)
-
-
-def mm_w(a, b):
-    return jnp.einsum("ri,ro->io", a, b, preferred_element_type=F32)
-
-
-def gather_rows(v):
-    return lax.all_gather(v, "shard", axis=0, tiled=True)
-
-
-def scatter_rows(v):
-    return lax.psum_scatter(v.astype(BF), "shard", scatter_dimension=0, tiled=True).astype(F32)
-
-
-def to_columns(w):
-    return lax.all_to_all(w, "shard", split_axis=1, concat_axis=0, tiled=True)
-
-
-def to_rows(g):
-    return lax.all_to_all(g, "shard", split_axis=0, concat_axis=1, tiled=True)
+    inverse = np.power(ROPE_BASE, -np.arange(middle) * 2.0 / head_width).astype(np.float32)
+    phases = np.arange(slot_len, dtype=np.float32)[:, None] * inverse
+    cosine = np.cos(phases.astype(np.float64))
+    sine = np.sin(phases.astype(np.float64))
+    table = np.concatenate([cosine, cosine, -sine, sine], axis=1)
+    return table.astype(np.float32)
 
 
 def shards(
@@ -306,155 +848,62 @@
     up_weight,
     down_weight,
 ):
-    shard_count = lax.axis_size("shard")
-    row_count = tokens.shape[1]
-    block_count = block_order.shape[1]
-    slot_len = row_count * shard_count
-    block_len = slot_len // block_count
-    head_width = query_gain.shape[0] * shard_count
-    score_scale = head_width ** (-0.5)
-    gains = lax.all_gather(
-        jnp.concatenate([norm1_gain, norm2_gain, query_gain, key_gain]), "shard", axis=0
+    S, R = lax.axis_size("shard"), lax.axis_size("replica")
+    at = lax.axis_index("shard")
+    z = layer_sizes(tokens[0], query_weight, key_weight, gate_weight, query_gain, S)
+    D, HD = z["D"], z["HD"]
+    gains = jnp.zeros((8, 2 * D + 2 * HD), F32)
+    start = 0
+    for g, full in ((norm1_gain, D), (norm2_gain, D), (query_gain, HD), (key_gain, HD)):
+        gains = lax.dynamic_update_slice(
+            gains, g.astype(F32)[None], (0, start + at * g.shape[0])
+        )
+        start += full
+    order = block_order[0]
+    count = order.shape[0]
+    place = jnp.arange(count, dtype=jnp.int32)
+    inverse = jnp.sum(jnp.where(order[None, :] == place[:, None], place[None, :], 0), axis=1)
+    meta = jnp.concatenate([order, inverse, lengths, jnp.zeros((15,), jnp.int32)])
+    table = jnp.asarray(rotary_table(z["T"], HD))
+    out, dx, gg, gd, ggu, go, gqkv = layer_call(
+        z, S, R,
+        (meta, tokens[0], cotangent[0], gains, table, query_weight, key_weight, value_weight,
+         output_weight, gate_weight, up_weight, down_weight),
     )
-    wide = norm1_gain.shape[0]
-    gain_one = gains[:, :wide].reshape(-1).astype(F32)
-    gain_two = gains[:, wide : 2 * wide].reshape(-1).astype(F32)
-    gain_query = gains[:, 2 * wide : 2 * wide + query_gain.shape[0]].reshape(-1).astype(F32)
-    gain_key = gains[:, 2 * wide + query_gain.shape[0] :].reshape(-1).astype(F32)
-    w_qkv = tuple(to_columns(w) for w in (query_weight, key_weight, value_weight))
-    w_gate, w_up = to_columns(gate_weight), to_columns(up_weight)
-    heads = w_qkv[0].shape[1] // head_width
-    kvs = w_qkv[1].shape[1] // head_width
-    per = heads // kvs
-
-    offsets = jnp.arange(slot_len, dtype=jnp.int32)
-    pos_all = (
-        jnp.repeat(block_order[0], block_len, total_repeat_length=slot_len) * block_len
-        + offsets % block_len
-    )
-    pos_local = lax.dynamic_slice_in_dim(pos_all, lax.axis_index("shard") * row_count, row_count)
-    valid_rows = (pos_local < lengths[0]).astype(F32)[:, None]
-    allowed = pos_all[None, None, None, :] <= pos_all[None, None, :, None]
-
-    inputs = tokens[0].astype(F32)
-    normed_f, norm_one_back = jax.vjp(rms_scale, inputs, gain_one)
-    normed = gather_rows(normed_f.astype(BF))
-    grad_result = cotangent[0].astype(F32) * valid_rows
-    grad_branch = gather_rows(grad_result.astype(BF))
-    query_raw = mm(normed, w_qkv[0]).reshape(slot_len, heads, head_width)
-    key_raw = mm(normed, w_qkv[1]).reshape(slot_len, kvs, head_width)
-    value = mm(normed, w_qkv[2]).astype(BF).reshape(slot_len, kvs, head_width)
-    cosine, sine = rotary_tables(pos_all, head_width)
-    cosine, sine = cosine[:, None, :], sine[:, None, :]
-
-    def turn(q, k, gq, gk):
-        return (
-            rotate_half(rms_scale(q, gq), cosine, sine),
-            rotate_half(rms_scale(k, gk), cosine, sine),
-        )
-
-    turned, turn_back = jax.vjp(turn, query_raw, key_raw, gain_query, gain_key)
-    query = turned[0].astype(BF).reshape(slot_len, kvs, per, head_width)
-    key = turned[1].astype(BF)
-
-    def scores_of():
-        raw = jnp.einsum("rkgd,tkd->kgrt", query, key, preferred_element_type=F32) * score_scale
-        return jnp.where(allowed, raw, -1e30)
-
-    scores = scores_of()
-    row_top = jnp.max(scores, axis=-1, keepdims=True)
-    log_total = row_top + jnp.log(jnp.sum(jnp.exp(scores - row_top), axis=-1, keepdims=True))
-    probs = jnp.exp(scores - log_total).astype(BF)
-    mixed = jnp.einsum("kgrt,tkd->rkgd", probs, value, preferred_element_type=F32)
-    mixed = mixed.reshape(slot_len, heads * head_width).astype(BF)
-    hidden = inputs + scatter_rows(mm(mixed, output_weight))
-    normed2_f, norm_two_back = jax.vjp(rms_scale, hidden, gain_two)
-    normed2 = gather_rows(normed2_f.astype(BF))
-    active_f, swish_back = jax.vjp(
-        lambda a, b: jax.nn.silu(a) * b, mm(normed2, w_gate), mm(normed2, w_up)
-    )
-    active = active_f.astype(BF)
-    output = (valid_rows * (hidden + scatter_rows(mm(active, down_weight)))).astype(BF)
-    grad_gate_f, grad_up_f = swish_back(mm_t(grad_branch, down_weight))
-    grad_gate, grad_up = grad_gate_f.astype(BF), grad_up_f.astype(BF)
-    grad_hidden_norm, grad_gain_two = norm_two_back(
-        scatter_rows(mm_t(grad_gate, w_gate) + mm_t(grad_up, w_up))
-    )
-    grad_hidden = grad_result + grad_hidden_norm
-    grad_mixed_in = gather_rows(grad_hidden.astype(BF))
-    grad_mixed = mm_t(grad_mixed_in, output_weight).astype(BF)
-    grad_mixed = grad_mixed.reshape(slot_len, kvs, per, head_width)
-    probs_f = jnp.exp(scores_of() - log_total)
-    grad_probs = jnp.einsum("rkgd,tkd->kgrt", grad_mixed, value, preferred_element_type=F32)
-    grad_value = jnp.einsum(
-        "kgrt,rkgd->tkd", probs_f.astype(BF), grad_mixed, preferred_element_type=F32
-    )
-    row_inner = jnp.sum(probs_f * grad_probs, axis=-1, keepdims=True)
-    grad_scores = (probs_f * (grad_probs - row_inner)).astype(BF)
-    grad_query = (
-        jnp.einsum("kgrt,tkd->rkgd", grad_scores, key, preferred_element_type=F32) * score_scale
-    )
-    grad_key = (
-        jnp.einsum("kgrt,rkgd->tkd", grad_scores, query, preferred_element_type=F32) * score_scale
-    )
-    grad_query_raw, grad_key_raw, grad_gain_query, grad_gain_key = turn_back(
-        (grad_query.reshape(slot_len, heads, head_width), grad_key)
-    )
-    grad_query_b = grad_query_raw.reshape(slot_len, -1).astype(BF)
-    grad_key_b = grad_key_raw.reshape(slot_len, -1).astype(BF)
-    grad_value_b = grad_value.reshape(slot_len, -1).astype(BF)
-    grad_normed = (
-        mm_t(grad_query_b, w_qkv[0]) + mm_t(grad_key_b, w_qkv[1]) + mm_t(grad_value_b, w_qkv[2])
-    )
-    grad_inputs_norm, grad_gain_one = norm_one_back(scatter_rows(grad_normed))
-    input_grad = grad_hidden + grad_inputs_norm
-
-    def part(left, right):
-        g = mm_w(left, right).astype(BF)
-        return g.reshape(shard_count, g.shape[0] // shard_count, g.shape[1])
-
-    share = {
-        "d": part(active, grad_branch),
-        "gu": part(normed2, jnp.concatenate([grad_gate, grad_up], axis=1)),
-        "o": part(mixed, grad_mixed_in),
-        "qkv": part(normed, jnp.concatenate([grad_query_b, grad_key_b, grad_value_b], axis=1)),
-    }
-    sums = dict(zip(ORDER, make(shard_count, lax.axis_size("replica"))(*[share[n] for n in ORDER])))
-    grad_down = sums["d"].astype(F32).reshape(-1, sums["d"].shape[-1])
-    grad_output_w = sums["o"].astype(F32).reshape(-1, sums["o"].shape[-1])
-
-    def columns(v, start, width):
-        v = v.reshape(v.shape[0], shard_count, -1)[:, :, start : start + width]
+    block = z["T"] // count
+    mine_blocks = lax.dynamic_slice_in_dim(order, at * (z["own"] // block), z["own"] // block)
+    position = mine_blocks[:, None] * block + jnp.arange(block, dtype=jnp.int32)[None, :]
+    valid = position.reshape(-1, 1) < lengths[0]
+    out = jnp.where(valid, out, jnp.zeros_like(out))
+    share = {"d": gd, "gu": ggu, "o": go, "qkv": gqkv}
+    share = {k: v.reshape(S, v.shape[0] // S, v.shape[1]) for k, v in share.items()}
+    sums = dict(zip(ORDER, make(S, R)(*[share[n] for n in ORDER])))
+    grad_down = sums["d"].astype(F32).reshape(-1, D)
+    grad_output_w = sums["o"].astype(F32).reshape(-1, D)
+
+    def columns(v, first, width):
+        v = v.reshape(v.shape[0], S, -1)[:, :, first : first + width]
         return v.reshape(v.shape[0], -1).astype(F32)
 
-    fw, qw, kw = w_gate.shape[1], w_qkv[0].shape[1], w_qkv[1].shape[1]
-    grad_gate_w = columns(sums["gu"], 0, fw)
-    grad_up_w = columns(sums["gu"], fw, fw)
-    grad_query_w = columns(sums["qkv"], 0, qw)
-    grad_key_w = columns(sums["qkv"], qw, kw)
-    grad_value_w = columns(sums["qkv"], qw + kw, kw)
-    small = jnp.concatenate([grad_gain_one, grad_gain_two, grad_gain_query, grad_gain_key])
-    small = lax.psum(small, ("shard", "replica"))
-    at = lax.axis_index("shard")
-    hw = query_gain.shape[0]
-
-    def own(start, size):
-        return lax.dynamic_slice_in_dim(small, start + at * size, size)
-
-    model = wide * shard_count
+    FW, QW, KW = z["FW"], z["QW"], z["KW"]
+    small = lax.psum(jnp.sum(gg, axis=0), ("shard", "replica"))
+
+    def mine(first, size):
+        return lax.dynamic_slice_in_dim(small, first + at * size, size)
+
     return (
-        output[None],
-        input_grad[None],
-        own(0, wide),
-        grad_query_w,
-        grad_key_w,
-        grad_value_w,
+        out[None],
+        dx[None],
+        mine(0, D // S),
+        columns(sums["qkv"], 0, QW),
+        columns(sums["qkv"], QW, KW),
+        columns(sums["qkv"], QW + KW, KW),
         grad_output_w,
-        own(2 * model, hw),
-        own(2 * model + head_width, hw),
-        own(model, wide),
-        grad_gate_w,
-        grad_up_w,
+        mine(2 * D, HD // S),
+        mine(2 * D + HD, HD // S),
+        mine(D, D // S),
+        columns(sums["gu"], 0, FW),
+        columns(sums["gu"], FW, FW),
         grad_down,
     )
 

time: 675 us -> 485 us (0.72)
  Pallas kernels: 213 us -> 398 us
  waiting for transfers between devices: 158 us -> 0 us
  matrix products: 94.5 us -> 0 us
  other arithmetic: 57.5 us -> 11.4 us
  local copies, waits for them, and re-layouts: 55.9 us -> 26.9 us
  starting transfers between devices: 21.4 us -> 0 us
  between operations: 16.5 us -> 1.84 us
  blocking collectives: 48 us -> 38.3 us
    pallas_call x0 -> x1, Pallas kernels: none -> 187 us  [layer_call(): pl.pallas_call(body, out_shape=[jax.ShapeDtypeStruct(*o) for o in outs],...]
    dot_general x24 -> x0, matrix products: 94.5 us -> none  [the longest x7 22.2 us: mm(): return jnp.einsum('ri,io->ro', a, b, preferred_element_type=F32)]
    all_to_all x5 -> x0, waiting for transfers between devices: 71.8 us -> none  [to_columns(): return lax.all_to_all(w, 'shard', split_axis=1, concat_axis=0, tiled=True)]
    reduce_scatter x4 -> x0, waiting for transfers between devices: 63.4 us -> none  [scatter_rows(): lax.psum_scatter(v.astype(BF), 'shard', scatter_dimension=0, tiled=True)]
    convert_element_type x12 -> x0, other arithmetic: 24.2 us -> none  [the longest x1 12.6 us: shards(): grad_scores = (probs_f * (grad_probs - row_inner)).astype(BF)]
    all_gather x4 -> x0, waiting for transfers between devices: 22.7 us -> none  [gather_rows(): return lax.all_gather(v, 'shard', axis=0, tiled=True)]
    all_to_all x5 -> x0, starting transfers between devices: 20.5 us -> none  [to_columns(): return lax.all_to_all(w, 'shard', split_axis=1, concat_axis=0, tiled=True)]
    unnamed x127 -> x18, local copies, waits for them, and re-layouts: 27.6 us -> 9.96 us
  transfers between devices with their start and end apart: 13 -> 0, of which waited for: 8 -> 0; matrix products, arithmetic and copies ran while one was open for 15% -> 0% of each run, Pallas kernels for 32% -> 0%
where the time goes in v3:
time: 485 us; the launch traced here: 477 us
  Pallas kernels  398 us (82%)
  blocking collectives  38.3 us (8%)
  local copies, waits for them, and re-layouts  26.9 us (6%)
  other arithmetic  11.4 us (2%)
    pallas_call x1, Pallas kernels, call(): pl.pallas_call(kern, out_shape=out_shape, in_specs=[any_] * 4, out_specs=...  211 us
    pallas_call x1, Pallas kernels, layer_call(): pl.pallas_call(body, out_shape=[jax.ShapeDtypeStruct(*o) for o in outs],...  187 us
    psum x1, blocking collectives, shards(): small = lax.psum(jnp.sum(gg, axis=0), ('shard', 'replica'))  38.3 us
    unnamed x18, local copies, waits for them, and re-layouts  9.96 us
    reshape x2, local copies, waits for them, and re-layouts, columns(): v = v.reshape(v.shape[0], S, -1)[:, :, first:first + width]  9.84 us

profile of v3, /device:TPU:0, one launch (start us, length us, event | category | flops | bytes accessed | tf_op | source)
XLA Modules:
  0.0 476.8 jit_solution(8940419496895617347)
XLA Ops:
  0.7 0.7 broadcast_in_dim.75
  1.3 0.6 broadcast_in_dim.63
  1.9 1.3 dynamic_update_slice.12
  3.3 0.7 broadcast_in_dim.76
  3.9 1.3 dynamic_update_slice.13
  5.3 0.7 bitcast_convert_fusion.3
  5.9 1.3 dynamic_update_slice.14
  7.2 0.7 bitcast_convert_fusion.2
  7.9 1.3 dynamic_update_slice.15.refs_3_
  9.9 0.8 select_reduce_fusion
  10.6 1.2 pad_add_fusion.refs_0_
  11.9 187.2 %layer.1 = (bf16[256,1024]{1,0:T(8,128)(2,1)}, f32[256,1024]{1,0:T(8,128)}, f32[8,2304]{1,0:T(8,128)}, bf16[768,1024]{1,0:T(8,128)(2,1)}, bf16[1024,1536]{1,0:T(...) custom-call(s32[32]{0:T(128)} %pad_add_fusion.refs_0_, bf16[256,1024]{1,0:T(8,128)(2,1)} %bitcast.55, ...), custom_call_target="tpu_custom_call" | custom-call | tf_op jit(solution)/shard_map/layer/pallas_call | solution.py:811
  199.0 211.1 %grad_sum.1 = (bf16[4,192,1024]{2,1,0:T(8,128)(2,1)}, bf16[256,6144]{1,0:T(8,128)(2,1)}, bf16[4,128,1024]{2,1,0:T(8,128)(2,1)}, bf16[256,4096]{1,0:T(8,128)(2,1)}) custom-call(bf16[4,192,1024]{2,1,0:T(8,128)(2,1)} %bitcast.50, bf16[4,256,1536]{2,1,0:T(8,128)(2,1)} %bitcast.47, bf16[4,128,1024]{2,1,0:T(8,128)(2,1)} %bitcast.51, bf16[4,256,1024]{2,1,0:T(8,128)(2,1)} %bitcast.49), custom_call_target="tpu_custom_call" | custom-call | tf_op jit(solution)/shard_map/grad_sum/pallas_call | solution.py:241
  410.2 6.5 %reshape.110 = bf16[256,4,1536]{2,1,0:T(4,128)(2,1)S(1)} reshape(bf16[256,6144]{1,0:T(8,128)(2,1)} %get-tuple-element.33) | data formatting | bytes 6291456 | tf_op jit(solution)/shard_map/reshape | solution.py:885
  416.7 1.2 slice_convert_fusion
  417.9 2.2 copy.32
  420.2 2.2 copy.33
  422.4 3.3 reshape.107
  425.7 0.3 slice_convert_fusion.2
  426.0 2.2 copy.29
  428.2 0.4 slice_convert_fusion.3
  428.6 0.0 copy-start
  428.6 1.2 copy.30
  429.8 1.2 copy.31
  430.9 0.0 copy-done
  430.9 0.0 copy-start.1
  430.9 2.2 bitcast_convert_fusion
  433.1 0.0 copy-start.4
  433.1 0.0 copy-start.5
  433.1 0.0 copy-start.3
  433.1 0.0 copy-done.1
  433.1 0.0 copy-start.2
  433.1 1.6 bitcast_convert_fusion.1
  434.8 0.0 copy-done.4
  434.8 38.3 %psum.7 = f32[2304]{0:T(1024)S(1)} all-reduce(f32[2304]{0:T(1024)S(1)} %reduce_sum.19), channel_id=1, replica_groups=mesh['shard'=4,'replica'=8] {'shard','replica'}, use_global_device_ids=true, to_apply=%region_2.3 | all-reduce | flops 2304 | bytes 18432 | tf_op jit(solution)/shard_map/psum | solution.py:889
  473.1 0.6 fusion
  473.8 0.6 fusion.1
  474.3 0.0 copy-done.5
  474.3 0.1 multiply_bitcast_fusion
  474.4 0.1 compare_bitcast_fusion
  474.5 0.0 copy-done.3
  474.5 0.9 select_bitcast_fusion
  475.4 0.0 copy-done.2
  475.4 1.0 copy.40
  (2 shorter events, 0.0 us)
Async XLA Ops:
  428.6 2.3 copy-start
  430.9 2.2 copy-start.1
  433.1 1.7 copy-start.4
  433.1 41.2 %copy-start.5 = (s32[1,8]{1,0:T(1,128)S(1)}, s32[1,8]{1,0:T(1,128)}, u32[]{:S(2)}) copy-start(s32[1,8]{1,0:T(1,128)} %param.19) | copy-start | bytes 100
  433.1 41.4 %copy-start.3 = (bf16[256,1024]{1,0:T(8,128)(2,1)S(1)}, bf16[256,1024]{1,0:T(8,128)(2,1)}, u32[]{:S(2)}) copy-start(bf16[256,1024]{1,0:T(8,128)(2,1)} %get-tuple-element.24) | copy-start | bytes 1572868
  433.1 42.3 %copy-start.2 = (f32[256,1024]{1,0:T(8,128)S(1)}, f32[256,1024]{1,0:T(8,128)}, u32[]{:S(2)}) copy-start(f32[256,1024]{1,0:T(8,128)} %get-tuple-element.25) | copy-start | bytes 3145732
